TPU v7x, 512 devices: a whole 4x8x8 slice. The times are simulated.
512 devices in a mesh: seq: 64 (over y, x, core), ch: 8 (over z).
Axes of the slice: x: 4, y: 8, z: 8, core: 2. Of those that a mesh axis runs over, the one named last changes fastest.
Arguments:
- inputs: bfloat16 [32768, 1024], P('seq', 'ch'), may hold values from -6 to 6
- conv_weight: bfloat16 [3, 1024], P(None, 'ch'), may hold values from -3 to 3
- mixing: bfloat16 [8, 512, 64, 128], P(None, 'seq'), may hold values from -0.5 to 0.5
- pattern: int32 [2, 512], P(None, 'seq'), may hold values from 0 to 7, as said below
- w_in: bfloat16 [1024, 4096], P(None, 'ch'), may hold values from -0.1875 to 0.1875
- w_out: bfloat16 [4096, 1024], P('ch'), may hold values from -0.09375 to 0.09375
- cotangent: bfloat16 [32768, 1024], P('seq', 'ch'), may hold values from -6 to 6
Outputs:
- layer_out: bfloat16 [32768, 1024], P('seq', 'ch')
- convolved: bfloat16 [32768, 1024], P('seq', 'ch')
- grad_input: bfloat16 [32768, 1024], P('seq', 'ch')
Inputs may be any that keep to these rules, and one draw needn't show every extreme that they name: `pattern`: for each of the 2 factors and each aligned run of 8 blocks (the blocks of one device), entry j of the run is a number k != j with entry k equal to j.
All inputs are finite; a program needn't handle non-finite values.
Results may differ from a plain program's by a relative error of at most 0.025.
Values may be sent and summed in bfloat16 or wider, within the bound.
A program may use at most 64 MiB of HBM per device.

v0:
```python
import jax
import jax.numpy as jnp
from jax import lax
from jax.sharding import PartitionSpec as P

BLOCK = 64
LOCAL = 2


root_two_pi = 0.7978845608028654


def extended(cells, sides, width):
    for axis, dim in sides:
        count = lax.axis_size(axis)
        ends = count - 1
        head = lax.slice_in_dim(cells, 0, width, axis=dim)
        tail = lax.slice_in_dim(cells, cells.shape[dim] - width, cells.shape[dim], axis=dim)
        cells = jnp.concatenate(
            [
                lax.ppermute(tail, axis, [(i, (i + 1) % count) for i in range(ends)]),
                cells,
                lax.ppermute(head, axis, [((i + 1) % count, i) for i in range(ends)]),
            ],
            axis=dim,
        )
    return cells


def from_partner(block, axis, bit):
    count = lax.axis_size(axis)
    route = []
    for low in range(count):
        high = low | 1 << bit
        if high != low and high < count:
            route += [(low, high), (high, low)]
    return lax.ppermute(block, axis, route)


def copy_for_each(value, axis):
    copies = jnp.broadcast_to(value, (lax.axis_size(axis), *value.shape))
    return lax.all_to_all(copies, axis, split_axis=0, concat_axis=0, tiled=True)


def in_order(blocks, dim):
    blocks = jnp.moveaxis(blocks, 0, dim)
    shape = blocks.shape
    return blocks.reshape(*shape[:dim], shape[dim] * shape[dim + 1], *shape[dim + 2 :])


def collect(value, axis, dim):
    blocks = copy_for_each(value, axis)
    return in_order(blocks, dim)


def split_up(value, dim, count):
    before, after = (value.shape[:dim], value.shape[dim + 1 :])
    return jnp.moveaxis(value.reshape(*before, count, -1, *after), dim, 0)


def summed_on_arrival(value, axis, dim):
    count = lax.axis_size(axis)
    blocks = lax.all_to_all(split_up(value, dim, count), axis, 0, 0, tiled=True)
    return jnp.sum(blocks, axis=0)


def gelu_grad(hidden):
    inner_arg = root_two_pi * (hidden + 0.044715 * hidden * hidden * hidden)
    tanh_val = jnp.tanh(inner_arg)
    slope = root_two_pi * (1.0 + 3.0 * 0.044715 * hidden * hidden)
    return 0.5 * (1.0 + tanh_val) + 0.5 * hidden * (1.0 - tanh_val * tanh_val) * slope


def on_device(inputs, conv_weight, mixing, pattern, w_in, w_out, cotangent):
    row_count, chan_count = inputs.shape
    blocks = row_count // BLOCK
    levels = lax.axis_size("seq").bit_length() - 1
    taps = conv_weight.astype(jnp.float32)
    padded = extended(inputs, (("seq", 0),), 1).astype(jnp.float32)
    convolved = (taps[0] * padded[:-2] + taps[1] * padded[1:-1] + taps[2] * padded[2:]).astype(
        jnp.bfloat16
    )
    state = convolved.reshape(blocks, BLOCK, chan_count)
    for factor in range(LOCAL + levels):
        weights = mixing[factor]
        if factor < LOCAL:
            mates = jnp.take(state, pattern[factor], axis=0)
        else:
            mates = from_partner(state, "seq", factor - LOCAL)
        updated = jnp.einsum(
            "bij,bjd->bid", weights[:, :, :BLOCK], state, preferred_element_type=jnp.float32
        )
        updated = updated + jnp.einsum(
            "bij,bjd->bid", weights[:, :, BLOCK:], mates, preferred_element_type=jnp.float32
        )
        state = updated.astype(jnp.bfloat16)
    mixed = state.reshape(row_count, chan_count)
    rows_in = w_in
    hidden = jnp.dot(collect(mixed, "ch", 1), rows_in, preferred_element_type=jnp.float32)
    activation = jax.nn.gelu(hidden, approximate=True).astype(jnp.bfloat16)
    cols_out = w_out
    branch = lax.psum_scatter(
        lax.dot_general(
            cols_out, activation, (((0,), (1,)), ((), ())), preferred_element_type=jnp.float32
        ),
        "ch",
        scatter_dimension=0,
        tiled=True,
    ).T
    layer_out = (mixed.astype(jnp.float32) + branch).astype(jnp.bfloat16)
    cols_out = w_out
    grad_act = lax.dot_general(
        lax.all_gather(cotangent, "ch", axis=1, tiled=True),
        cols_out,
        (((1,), (1,)), ((), ())),
        preferred_element_type=jnp.float32,
    )
    grad_hidden = (grad_act * gelu_grad(hidden)).astype(jnp.bfloat16)
    rows_in = w_in
    summed = summed_on_arrival(
        lax.dot_general(
            rows_in, grad_hidden, (((1,), (1,)), ((), ())), preferred_element_type=jnp.float32
        ),
        "ch",
        0,
    ).T
    grad_mixed = (cotangent.astype(jnp.float32) + summed).astype(jnp.bfloat16)
    grads = grad_mixed.reshape(blocks, BLOCK, chan_count)
    for factor in reversed(range(LOCAL + levels)):
        weights = mixing[factor]
        own_term = jnp.einsum(
            "bji,bjd->bid", weights[:, :, :BLOCK], grads, preferred_element_type=jnp.float32
        )
        if factor < LOCAL:
            cross_term = jnp.einsum(
                "bji,bjd->bid", weights[:, :, BLOCK:], grads, preferred_element_type=jnp.float32
            )
            combined = own_term + jnp.take(cross_term, pattern[factor], axis=0)
        else:
            cross_term = jnp.einsum(
                "bji,bjd->bid", weights[:, :, BLOCK:], grads, preferred_element_type=jnp.float32
            )
            combined = own_term + from_partner(cross_term, "seq", factor - LOCAL)
        grads = combined.astype(jnp.bfloat16)
    grad_pad = extended(grads.reshape(row_count, chan_count), (("seq", 0),), 1).astype(jnp.float32)
    grad_input = (
        taps[0] * grad_pad[2:] + taps[1] * grad_pad[1:-1] + taps[2] * grad_pad[:-2]
    ).astype(jnp.bfloat16)
    return (layer_out, convolved, grad_input)


def solution(mesh):
    return jax.shard_map(
        on_device,
        mesh=mesh,
        in_specs=(
            P("seq", "ch"),
            P(None, "ch"),
            P(None, "seq", None, None),
            P(None, "seq"),
            P(None, "ch"),
            P("ch", None),
            P("seq", "ch"),
        ),
        out_specs=(P("seq", "ch"), P("seq", "ch"), P("seq", "ch")),
        check_vma=False,
    )
```

profile of v0, /device:TPU:1, one launch (start us, length us, event | category | flops | bytes accessed | tf_op | source)
XLA Modules:
  0.0 268.8 jit_solution(3407165750593198803)
XLA Ops:
  7.2 0.8 fusion.115
  8.0 8.7 %collective-permute-start.1 = (bf16[1,128]{1,0:T(2,128)(2,1)S(1)}, bf16[1,128]{1,0:T(2,128)(2,1)S(1)}, u32[]{:S(2)}, u32[]{:S(2)}) collective-permute-start(bf16[1,128]{1,0:T(2,128)(2,1)S(1)} %get-tuple-element.20), channel_id=1, source_target_pairs={{8,0},{16,8},{24,16},{32,24},{40,32},{48,40},{56,48},{64,56},{72,6... | collective-permute-start | bytes 776 | tf_op jit(solution)/shard_map/ppermute | solution.py:23
  16.8 1.9 collective-permute-start
  18.7 0.7 convert_element_type.105
  19.4 1.4 slice_bitcast_fusion
  22.2 0.6 gather_fusion.1
  23.1 2.4 collective-permute-start.2
  25.7 0.8 collective-permute-done.2
  26.7 2.3 collective-permute-start.3
  29.2 4.1 %collective-permute-done.3 = bf16[8,64,128]{2,1,0:T(8,128)(2,1)S(1)} collective-permute-done((bf16[8,64,128]{2,1,0:T(8,128)(2,1)S(1)}, bf16[8,64,128]{2,1,0:T(8,128)(2,1)S(1)}, u32[]{:S(2)}, u32[]{:S(2)}) %collective-permute-start.3) | collective-permute-done | bytes 131104 | tf_op jit(solution)/shard_map/ppermute | solution.py:37
  33.5 2.3 collective-permute-start.4
  36.0 4.7 %collective-permute-done.4 = bf16[8,64,128]{2,1,0:T(8,128)(2,1)S(1)} collective-permute-done((bf16[8,64,128]{2,1,0:T(8,128)(2,1)S(1)}, bf16[8,64,128]{2,1,0:T(8,128)(2,1)S(1)}, u32[]{:S(2)}, u32[]{:S(2)}) %collective-permute-start.4) | collective-permute-done | bytes 131104 | tf_op jit(solution)/shard_map/ppermute | solution.py:37
  41.0 2.3 collective-permute-start.5
  43.5 3.2 %collective-permute-done.5 = bf16[8,64,128]{2,1,0:T(8,128)(2,1)S(1)} collective-permute-done((bf16[8,64,128]{2,1,0:T(8,128)(2,1)S(1)}, bf16[8,64,128]{2,1,0:T(8,128)(2,1)S(1)}, u32[]{:S(2)}, u32[]{:S(2)}) %collective-permute-start.5) | collective-permute-done | bytes 131104 | tf_op jit(solution)/shard_map/ppermute | solution.py:37
  47.0 3.3 %collective-permute-start.6 = (bf16[8,64,128]{2,1,0:T(8,128)(2,1)S(1)}, bf16[8,64,128]{2,1,0:T(8,128)(2,1)S(1)}, u32[]{:S(2)}, u32[]{:S(2)}) collective-permute-start(bf16[8,64,128]{2,1,0:T(8,128)(2,1)S(1)} %bitcast.175), channel_id=1, source_target_pairs={{0,128},{128,0},{8,136},{136,8},{16,144},{144,16},{24,152},{152,24... | collective-permute-start | bytes 393224 | tf_op jit(solution)/shard_map/ppermute | solution.py:37
  50.4 4.5 %collective-permute-done.6 = bf16[8,64,128]{2,1,0:T(8,128)(2,1)S(1)} collective-permute-done((bf16[8,64,128]{2,1,0:T(8,128)(2,1)S(1)}, bf16[8,64,128]{2,1,0:T(8,128)(2,1)S(1)}, u32[]{:S(2)}, u32[]{:S(2)}) %collective-permute-start.6) | collective-permute-done | bytes 131104 | tf_op jit(solution)/shard_map/ppermute | solution.py:37
  55.2 7.5 %collective-permute-start.7 = (bf16[8,64,128]{2,1,0:T(8,128)(2,1)S(1)}, bf16[8,64,128]{2,1,0:T(8,128)(2,1)S(1)}, u32[]{:S(2)}, u32[]{:S(2)}) collective-permute-start(bf16[8,64,128]{2,1,0:T(8,128)(2,1)S(1)} %bitcast.171), channel_id=1, source_target_pairs={{0,256},{256,0},{8,264},{264,8},{16,272},{272,16},{24,280},{280,24... | collective-permute-start | bytes 393224 | tf_op jit(solution)/shard_map/ppermute | solution.py:37
  62.9 2.2 collective-permute-done.7
  65.5 1.1 broadcast_in_dim.21
  66.6 10.0 %all-to-all-start = ((bf16[8,512,128]{1,2,0:T(8,128)(2,1)}), bf16[8,512,128]{1,2,0:T(8,128)(2,1)S(1)}, u32[]{:S(2)}, u32[]{:S(2)}) async-start(bf16[8,512,128]{1,2,0:T(8,128)(2,1)} %broadcast_in_dim.21), calls=%async_computation | async-start | bytes 2097152 | tf_op jit(solution)/shard_map/all_to_all | solution.py:42
  76.7 0.7 all-gather.2.cloned.1.call-update
  77.4 24.4 %all-to-all-done = bf16[8,512,128]{1,2,0:T(8,128)(2,1)S(1)} async-done(((bf16[8,512,128]{1,2,0:T(8,128)(2,1)}), bf16[8,512,128]{1,2,0:T(8,128)(2,1)S(1)}, u32[]{:S(2)}, u32[]{:S(2)}) %all-to-all-start) | async-done | bytes 1048608 | tf_op jit(solution)/shard_map/all_to_all | solution.py:42
  101.8 3.0 %fusion.116 = f32[512,512]{1,0:T(8,128)} fusion(bf16[512,1024]{0,1:T(8,128)(2,1)S(1)} %bitcast.168, bf16[1024,512]{1,0:T(8,128)(2,1)} %param.15), kind=kOutput, calls=%fused_computation.177 | convolution fusion | flops 536870912 | bytes 3145728 | tf_op jit(solution)/shard_map/dot_general | solution.py:99
  104.8 19.5 %all-gather.2.cloned.1.call-done = bf16[512,1024]{1,0:T(8,128)(2,1)} async-done(((bf16[512,128]{1,0:T(8,128)(2,1)}), bf16[512,1024]{1,0:T(8,128)(2,1)}) %all-gather.2.cloned.1.call-update) | async-done | bytes 1048592 | tf_op jit(solution)/shard_map/all_gather | solution.py:113
  124.3 3.6 %convolution_bitcast_fusion = f32[64,8,8,128]{3,2,1,0:T(8,128)S(1)} fusion(bf16[1024,512]{1,0:T(8,128)(2,1)} %param.15, bf16[512,1024]{1,0:T(8,128)(2,1)} %all-gather.2.cloned.1.call-done, bf16[512,1024]{1,0:T(8,128)(2,1)S(1)} %copy-done, f32[512,512]{1,0:T(8,128)} %fusion.116), kind=kOutput, calls=%fused_computation.5 | convolution fusion | flops 1078722560 | bytes 6291456 | tf_op jit(solution)/shard_map/dot_general | solution.py:121
  128.0 49.7 %all_to_all.10 = f32[8,128,512]{1,2,0:T(8,128)S(1)} all-to-all(f32[8,128,512]{1,2,0:T(8,128)S(1)} %bitcast.161), channel_id=1, replica_groups=mesh['seq'=64,'ch'=8] {'ch'}, dimensions={0} | all-to-all | bytes 4194304 | tf_op jit(solution)/shard_map/all_to_all | solution.py:63
  177.7 0.8 reduce_sum.9
  178.6 1.1 fusion.55
  179.7 1.2 convolution_bitcast_fusion.16
  180.9 7.2 %collective-permute-start.8 = (f32[8,64,128]{2,1,0:T(8,128)S(1)}, f32[8,64,128]{2,1,0:T(8,128)S(1)}, u32[]{:S(2)}, u32[]{:S(2)}) collective-permute-start(f32[8,64,128]{2,1,0:T(8,128)S(1)} %convolution_bitcast_fusion.16), channel_id=1, source_target_pairs={{0,256},{256,0},{8,264},{264,8},{16,272},{272,16},{24,280},{280,24... | collective-permute-start | bytes 786440 | tf_op jit(solution)/shard_map/ppermute | solution.py:37
  188.1 6.4 %collective-permute-done.8 = f32[8,64,128]{2,1,0:T(8,128)S(1)} collective-permute-done((f32[8,64,128]{2,1,0:T(8,128)S(1)}, f32[8,64,128]{2,1,0:T(8,128)S(1)}, u32[]{:S(2)}, u32[]{:S(2)}) %collective-permute-start.8) | collective-permute-done | bytes 262176 | tf_op jit(solution)/shard_map/ppermute | solution.py:37
  194.5 1.1 fusion.9
  195.7 1.2 convolution_bitcast_fusion.14
  196.9 2.3 collective-permute-start.9
  199.1 2.2 convolution_bitcast_fusion.1
  201.3 7.1 %collective-permute-done.9 = f32[8,64,128]{2,1,0:T(8,128)S(1)} collective-permute-done((f32[8,64,128]{2,1,0:T(8,128)S(1)}, f32[8,64,128]{2,1,0:T(8,128)S(1)}, u32[]{:S(2)}, u32[]{:S(2)}) %collective-permute-start.9) | collective-permute-done | bytes 262176 | tf_op jit(solution)/shard_map/ppermute | solution.py:37
  209.0 2.1 collective-permute-start.10
  211.0 5.9 %collective-permute-done.10 = f32[8,64,128]{2,1,0:T(8,128)S(1)} collective-permute-done((f32[8,64,128]{2,1,0:T(8,128)S(1)}, f32[8,64,128]{2,1,0:T(8,128)S(1)}, u32[]{:S(2)}, u32[]{:S(2)}) %collective-permute-start.10) | collective-permute-done | bytes 262176 | tf_op jit(solution)/shard_map/ppermute | solution.py:37
  217.5 5.9 %collective-permute-start.11 = (f32[8,64,128]{2,1,0:T(8,128)S(1)}, f32[8,64,128]{2,1,0:T(8,128)S(1)}, u32[]{:S(2)}, u32[]{:S(2)}) collective-permute-start(f32[8,64,128]{2,1,0:T(8,128)S(1)} %convolution_bitcast_fusion.10), channel_id=1, source_target_pairs={{0,32},{32,0},{8,40},{40,8},{16,48},{48,16},{24,56},{56,24},{64,96... | collective-permute-start | bytes 786440 | tf_op jit(solution)/shard_map/ppermute | solution.py:37
  223.4 3.7 %collective-permute-done.11 = f32[8,64,128]{2,1,0:T(8,128)S(1)} collective-permute-done((f32[8,64,128]{2,1,0:T(8,128)S(1)}, f32[8,64,128]{2,1,0:T(8,128)S(1)}, u32[]{:S(2)}, u32[]{:S(2)}) %collective-permute-start.11) | collective-permute-done | bytes 262176 | tf_op jit(solution)/shard_map/ppermute | solution.py:37
  227.7 2.5 collective-permute-start.12
  230.3 7.5 %collective-permute-done.12 = f32[8,64,128]{2,1,0:T(8,128)S(1)} collective-permute-done((f32[8,64,128]{2,1,0:T(8,128)S(1)}, f32[8,64,128]{2,1,0:T(8,128)S(1)}, u32[]{:S(2)}, u32[]{:S(2)}) %collective-permute-start.12) | collective-permute-done | bytes 262176 | tf_op jit(solution)/shard_map/ppermute | solution.py:37
  238.4 11.9 %collective-permute-start.13 = (f32[8,64,128]{2,1,0:T(8,128)S(1)}, f32[8,64,128]{2,1,0:T(8,128)S(1)}, u32[]{:S(2)}, u32[]{:S(2)}) collective-permute-start(f32[8,64,128]{2,1,0:T(8,128)S(1)} %convolution_bitcast_fusion.6), channel_id=1, source_target_pairs={{0,8},{8,0},{16,24},{24,16},{32,40},{40,32},{48,56},{56,48},{64,72... | collective-permute-start | bytes 786440 | tf_op jit(solution)/shard_map/ppermute | solution.py:37
  250.2 1.1 collective-permute-done.13
  253.9 2.3 collective-permute-start.15
  256.2 3.3 %collective-permute-start.14 = (bf16[1,128]{1,0:T(2,128)(2,1)S(1)}, bf16[1,128]{1,0:T(2,128)(2,1)S(1)}, u32[]{:S(2)}, u32[]{:S(2)}) collective-permute-start(bf16[1,128]{1,0:T(2,128)(2,1)S(1)} %get-tuple-element.17), channel_id=1, source_target_pairs={{0,8},{8,16},{16,24},{24,32},{32,40},{40,48},{48,56},{56,64},{64,7... | collective-permute-start | bytes 776 | tf_op jit(solution)/shard_map/ppermute | solution.py:21
  259.6 1.6 fusion.56
  261.3 0.7 fusion.50
  (93 shorter events, 9.0 us)
Async XLA Ops:
  7.2 117.1 %copy-start = (bf16[512,1024]{1,0:T(8,128)(2,1)S(1)}, bf16[512,1024]{1,0:T(8,128)(2,1)}, u32[]{:S(2)}) copy-start(bf16[512,1024]{1,0:T(8,128)(2,1)} %param.16) | copy-start | bytes 3145732
  7.2 13.7 %copy-start.13 = (bf16[512,128]{1,0:T(8,128)(2,1)S(1)}, bf16[512,128]{1,0:T(8,128)(2,1)}, u32[]{:S(2)}) copy-start(bf16[512,128]{1,0:T(8,128)(2,1)} %param.11) | copy-start | bytes 393220
  7.2 13.6 %copy-start.20 = (s32[2,8]{1,0:T(2,128)S(1)}, s32[2,8]{1,0:T(2,128)}, u32[]{:S(2)}) copy-start(s32[2,8]{1,0:T(2,128)} %param.14) | copy-start | bytes 196
  8.0 12.9 %collective-permute-start.1 = (bf16[1,128]{1,0:T(2,128)(2,1)S(1)}, bf16[1,128]{1,0:T(2,128)(2,1)S(1)}, u32[]{:S(2)}, u32[]{:S(2)}) collective-permute-start(bf16[1,128]{1,0:T(2,128)(2,1)S(1)} %get-tuple-element.20), channel_id=1, source_target_pairs={{8,0},{16,8},{24,16},{32,24},{40,32},{48,40},{56,48},{64,56},{72,6... | collective-permute-start | bytes 776 | tf_op jit(solution)/shard_map/ppermute | solution.py:23
  16.8 4.1 %collective-permute-start = (bf16[1,128]{1,0:T(2,128)(2,1)S(1)}, bf16[1,128]{1,0:T(2,128)(2,1)S(1)}, u32[]{:S(2)}, u32[]{:S(2)}) collective-permute-start(bf16[1,128]{1,0:T(2,128)(2,1)S(1)} %get-tuple-element.19), channel_id=1, source_target_pairs={{0,8},{8,16},{16,24},{24,32},{32,40},{40,48},{48,56},{56,64},{64,7... | collective-permute-start | bytes 776 | tf_op jit(solution)/shard_map/ppermute | solution.py:21
  19.4 2.4 copy-start.14
  20.8 2.3 copy-start.6
  20.8 2.3 copy-start.8
  20.8 25.9 %copy-start.1 = (bf16[8,64,128]{2,1,0:T(8,128)(2,1)}, bf16[8,64,128]{2,1,0:T(8,128)(2,1)S(1)}, u32[]{:S(2)}) copy-start(bf16[8,64,128]{2,1,0:T(8,128)(2,1)S(1)} %get-tuple-element.10) | copy-start | bytes 393220
  20.8 45.8 %copy-start.3 = (bf16[8,64,128]{2,1,0:T(8,128)(2,1)}, bf16[8,64,128]{2,1,0:T(8,128)(2,1)S(1)}, u32[]{:S(2)}) copy-start(bf16[8,64,128]{2,1,0:T(8,128)(2,1)S(1)} %get-tuple-element.16) | copy-start | bytes 393220
  20.8 45.8 %copy-start.5 = (bf16[8,64,128]{2,1,0:T(8,128)(2,1)}, bf16[8,64,128]{2,1,0:T(8,128)(2,1)S(1)}, u32[]{:S(2)}) copy-start(bf16[8,64,128]{2,1,0:T(8,128)(2,1)S(1)} %get-tuple-element.9) | copy-start | bytes 393220
  20.8 2.2 copy-start.16
  20.9 2.2 copy-start.18
  21.1 8.1 %copy-start.12 = (bf16[512,128]{1,0:T(8,128)(2,1)}, bf16[512,128]{1,0:T(8,128)(2,1)S(1)}, u32[]{:S(2)}) copy-start(bf16[512,128]{1,0:T(8,128)(2,1)S(1)} %fusion.53) | copy-start | bytes 393220
  23.1 3.4 %collective-permute-start.2 = (bf16[8,64,128]{2,1,0:T(8,128)(2,1)S(1)}, bf16[8,64,128]{2,1,0:T(8,128)(2,1)S(1)}, u32[]{:S(2)}, u32[]{:S(2)}) collective-permute-start(bf16[8,64,128]{2,1,0:T(8,128)(2,1)S(1)} %bitcast.176), channel_id=1, source_target_pairs={{0,8},{8,0},{16,24},{24,16},{32,40},{40,32},{48,56},{56,48},{64,72... | collective-permute-start | bytes 393224 | tf_op jit(solution)/shard_map/ppermute | solution.py:37
  26.7 6.6 %collective-permute-start.3 = (bf16[8,64,128]{2,1,0:T(8,128)(2,1)S(1)}, bf16[8,64,128]{2,1,0:T(8,128)(2,1)S(1)}, u32[]{:S(2)}, u32[]{:S(2)}) collective-permute-start(bf16[8,64,128]{2,1,0:T(8,128)(2,1)S(1)} %bitcast.172), channel_id=1, source_target_pairs={{0,16},{16,0},{8,24},{24,8},{32,48},{48,32},{40,56},{56,40},{64,80... | collective-permute-start | bytes 393224 | tf_op jit(solution)/shard_map/ppermute | solution.py:37
  33.5 7.2 %collective-permute-start.4 = (bf16[8,64,128]{2,1,0:T(8,128)(2,1)S(1)}, bf16[8,64,128]{2,1,0:T(8,128)(2,1)S(1)}, u32[]{:S(2)}, u32[]{:S(2)}) collective-permute-start(bf16[8,64,128]{2,1,0:T(8,128)(2,1)S(1)} %bitcast.173), channel_id=1, source_target_pairs={{0,32},{32,0},{8,40},{40,8},{16,48},{48,16},{24,56},{56,24},{64,96... | collective-permute-start | bytes 393224 | tf_op jit(solution)/shard_map/ppermute | solution.py:37
  41.0 5.7 %collective-permute-start.5 = (bf16[8,64,128]{2,1,0:T(8,128)(2,1)S(1)}, bf16[8,64,128]{2,1,0:T(8,128)(2,1)S(1)}, u32[]{:S(2)}, u32[]{:S(2)}) collective-permute-start(bf16[8,64,128]{2,1,0:T(8,128)(2,1)S(1)} %bitcast.174), channel_id=1, source_target_pairs={{0,64},{64,0},{8,72},{72,8},{16,80},{80,16},{24,88},{88,24},{32,96... | collective-permute-start | bytes 393224 | tf_op jit(solution)/shard_map/ppermute | solution.py:37
  47.0 8.0 %collective-permute-start.6 = (bf16[8,64,128]{2,1,0:T(8,128)(2,1)S(1)}, bf16[8,64,128]{2,1,0:T(8,128)(2,1)S(1)}, u32[]{:S(2)}, u32[]{:S(2)}) collective-permute-start(bf16[8,64,128]{2,1,0:T(8,128)(2,1)S(1)} %bitcast.175), channel_id=1, source_target_pairs={{0,128},{128,0},{8,136},{136,8},{16,144},{144,16},{24,152},{152,24... | collective-permute-start | bytes 393224 | tf_op jit(solution)/shard_map/ppermute | solution.py:37
  55.2 9.9 %collective-permute-start.7 = (bf16[8,64,128]{2,1,0:T(8,128)(2,1)S(1)}, bf16[8,64,128]{2,1,0:T(8,128)(2,1)S(1)}, u32[]{:S(2)}, u32[]{:S(2)}) collective-permute-start(bf16[8,64,128]{2,1,0:T(8,128)(2,1)S(1)} %bitcast.171), channel_id=1, source_target_pairs={{0,256},{256,0},{8,264},{264,8},{16,272},{272,16},{24,280},{280,24... | collective-permute-start | bytes 393224 | tf_op jit(solution)/shard_map/ppermute | solution.py:37
  65.4 39.4 %copy-start.10 = (bf16[8,128,64]{1,2,0:T(8,128)(2,1)}, bf16[8,128,64]{1,2,0:T(8,128)(2,1)S(1)}, u32[]{:S(2)}) copy-start(bf16[8,128,64]{1,2,0:T(8,128)(2,1)S(1)} %fusion.24) | copy-start | bytes 393220
  66.6 35.2 %all-to-all-start = ((bf16[8,512,128]{1,2,0:T(8,128)(2,1)}), bf16[8,512,128]{1,2,0:T(8,128)(2,1)S(1)}, u32[]{:S(2)}, u32[]{:S(2)}) async-start(bf16[8,512,128]{1,2,0:T(8,128)(2,1)} %broadcast_in_dim.21), calls=%async_computation | async-start | bytes 2097152 | tf_op jit(solution)/shard_map/all_to_all | solution.py:42
  76.6 47.6 %all-gather.2.cloned.1.call-start = ((), (), s32[]{:S(2)}) async-start(), calls=%async_computation.4 | async-start | bytes 1179648 | tf_op jit(solution)/shard_map/all_gather | solution.py:113
  77.4 182.2 %reduce-scatter.2.cloned.1.call-start = ((), (), s32[]{:S(2)}) async-start(), calls=%async_computation.3 | async-start | bytes 2359296 | tf_op jit(solution)/shard_map/reduce_scatter | solution.py:102
  178.6 20.6 %copy-start.21 = (f32[512,512]{1,0:T(8,128)S(1)}, f32[512,512]{1,0:T(8,128)}, u32[]{:S(2)}) copy-start(f32[512,512]{1,0:T(8,128)} %fusion.116) | copy-start | bytes 3145732
  180.9 13.6 %collective-permute-start.8 = (f32[8,64,128]{2,1,0:T(8,128)S(1)}, f32[8,64,128]{2,1,0:T(8,128)S(1)}, u32[]{:S(2)}, u32[]{:S(2)}) collective-permute-start(f32[8,64,128]{2,1,0:T(8,128)S(1)} %convolution_bitcast_fusion.16), channel_id=1, source_target_pairs={{0,256},{256,0},{8,264},{264,8},{16,272},{272,16},{24,280},{280,24... | collective-permute-start | bytes 786440 | tf_op jit(solution)/shard_map/ppermute | solution.py:37
  196.9 11.5 %collective-permute-start.9 = (f32[8,64,128]{2,1,0:T(8,128)S(1)}, f32[8,64,128]{2,1,0:T(8,128)S(1)}, u32[]{:S(2)}, u32[]{:S(2)}) collective-permute-start(f32[8,64,128]{2,1,0:T(8,128)S(1)} %convolution_bitcast_fusion.14), channel_id=1, source_target_pairs={{0,128},{128,0},{8,136},{136,8},{16,144},{144,16},{24,152},{152,24... | collective-permute-start | bytes 786440 | tf_op jit(solution)/shard_map/ppermute | solution.py:37
  201.3 7.1 %copy-start.4 = (bf16[8,64,128]{2,1,0:T(8,128)(2,1)S(1)}, bf16[8,64,128]{2,1,0:T(8,128)(2,1)}, u32[]{:S(2)}) copy-start(bf16[8,64,128]{2,1,0:T(8,128)(2,1)} %copy-done.3) | copy-start | bytes 393220
  201.3 7.4 %copy-start.2 = (bf16[8,64,128]{2,1,0:T(8,128)(2,1)S(1)}, bf16[8,64,128]{2,1,0:T(8,128)(2,1)}, u32[]{:S(2)}) copy-start(bf16[8,64,128]{2,1,0:T(8,128)(2,1)} %copy-done.1) | copy-start | bytes 393220
  209.0 42.7 %copy-start.9 = (bf16[8,64,128]{2,1,0:T(8,128)(2,1)S(1)}, bf16[8,64,128]{2,1,0:T(8,128)(2,1)}, u32[]{:S(2)}) copy-start(bf16[8,64,128]{2,1,0:T(8,128)(2,1)} %copy-done.8) | copy-start | bytes 393220
  209.0 8.0 %collective-permute-start.10 = (f32[8,64,128]{2,1,0:T(8,128)S(1)}, f32[8,64,128]{2,1,0:T(8,128)S(1)}, u32[]{:S(2)}, u32[]{:S(2)}) collective-permute-start(f32[8,64,128]{2,1,0:T(8,128)S(1)} %convolution_bitcast_fusion.12), channel_id=1, source_target_pairs={{0,64},{64,0},{8,72},{72,8},{16,80},{80,16},{24,88},{88,24},{32,96... | collective-permute-start | bytes 786440 | tf_op jit(solution)/shard_map/ppermute | solution.py:37
  217.5 35.0 %copy-start.19 = (pred[8]{0:T(512)(128)(4,1)S(1)}, pred[8]{0:T(512)(128)(4,1)}, u32[]{:S(2)}) copy-start(pred[8]{0:T(512)(128)(4,1)} %copy-done.18) | copy-start | bytes 28
  217.5 9.7 %collective-permute-start.11 = (f32[8,64,128]{2,1,0:T(8,128)S(1)}, f32[8,64,128]{2,1,0:T(8,128)S(1)}, u32[]{:S(2)}, u32[]{:S(2)}) collective-permute-start(f32[8,64,128]{2,1,0:T(8,128)S(1)} %convolution_bitcast_fusion.10), channel_id=1, source_target_pairs={{0,32},{32,0},{8,40},{40,8},{16,48},{48,16},{24,56},{56,24},{64,96... | collective-permute-start | bytes 786440 | tf_op jit(solution)/shard_map/ppermute | solution.py:37
  227.4 25.4 %copy-start.7 = (bf16[8,64,128]{2,1,0:T(8,128)(2,1)S(1)}, bf16[8,64,128]{2,1,0:T(8,128)(2,1)}, u32[]{:S(2)}) copy-start(bf16[8,64,128]{2,1,0:T(8,128)(2,1)} %copy-done.6) | copy-start | bytes 393220
  227.7 10.1 %collective-permute-start.12 = (f32[8,64,128]{2,1,0:T(8,128)S(1)}, f32[8,64,128]{2,1,0:T(8,128)S(1)}, u32[]{:S(2)}, u32[]{:S(2)}) collective-permute-start(f32[8,64,128]{2,1,0:T(8,128)S(1)} %convolution_bitcast_fusion.8), channel_id=1, source_target_pairs={{0,16},{16,0},{8,24},{24,8},{32,48},{48,32},{40,56},{56,40},{64,80... | collective-permute-start | bytes 786440 | tf_op jit(solution)/shard_map/ppermute | solution.py:37
  238.0 15.6 %copy-start.17 = (pred[8]{0:T(512)(128)(4,1)S(1)}, pred[8]{0:T(512)(128)(4,1)}, u32[]{:S(2)}) copy-start(pred[8]{0:T(512)(128)(4,1)} %copy-done.16) | copy-start | bytes 28
  238.4 21.2 %copy-start.11 = (bf16[8,128,64]{1,2,0:T(8,128)(2,1)S(1)}, bf16[8,128,64]{1,2,0:T(8,128)(2,1)}, u32[]{:S(2)}) copy-start(bf16[8,128,64]{1,2,0:T(8,128)(2,1)} %copy-done.10) | copy-start | bytes 393220
  238.4 13.0 %collective-permute-start.13 = (f32[8,64,128]{2,1,0:T(8,128)S(1)}, f32[8,64,128]{2,1,0:T(8,128)S(1)}, u32[]{:S(2)}, u32[]{:S(2)}) collective-permute-start(f32[8,64,128]{2,1,0:T(8,128)S(1)} %convolution_bitcast_fusion.6), channel_id=1, source_target_pairs={{0,8},{8,0},{16,24},{24,16},{32,40},{40,32},{48,56},{56,48},{64,72... | collective-permute-start | bytes 786440 | tf_op jit(solution)/shard_map/ppermute | solution.py:37
  251.6 9.6 %copy-start.15 = (f32[128]{0:T(128)S(1)}, f32[128]{0:T(128)}, u32[]{:S(2)}) copy-start(f32[128]{0:T(128)} %copy-done.14) | copy-start | bytes 1540
  253.9 7.3 %collective-permute-start.15 = (bf16[1,128]{1,0:T(2,128)(2,1)S(1)}, bf16[1,128]{1,0:T(2,128)(2,1)S(1)}, u32[]{:S(2)}, u32[]{:S(2)}) collective-permute-start(bf16[1,128]{1,0:T(2,128)(2,1)S(1)} %get-tuple-element.18), channel_id=1, source_target_pairs={{8,0},{16,8},{24,16},{32,24},{40,32},{48,40},{56,48},{64,56},{72,6... | collective-permute-start | bytes 776 | tf_op jit(solution)/shard_map/ppermute | solution.py:23
  256.2 5.0 %collective-permute-start.14 = (bf16[1,128]{1,0:T(2,128)(2,1)S(1)}, bf16[1,128]{1,0:T(2,128)(2,1)S(1)}, u32[]{:S(2)}, u32[]{:S(2)}) collective-permute-start(bf16[1,128]{1,0:T(2,128)(2,1)S(1)} %get-tuple-element.17), channel_id=1, source_target_pairs={{0,8},{8,16},{16,24},{24,32},{32,40},{40,48},{48,56},{56,64},{64,7... | collective-permute-start | bytes 776 | tf_op jit(solution)/shard_map/ppermute | solution.py:21
Sparse Core Ops, SparseCore 0:
  79.4 44.7 all-gather.1
  201.5 45.2 reduce-scatter.1
where the time goes:
time: 272 us; the launch traced here: 269 us
  waiting for transfers between devices  96 us (35%)
  starting transfers between devices  78.3 us (29%)
  blocking collectives  49.7 us (18%)
  matrix products  18.9 us (7%)
  between operations  14.8 us (5%)
  local copies, waits for them, and re-layouts  5.94 us (2%)
  other arithmetic  5.17 us (2%)
    ppermute x12, starting transfers between devices, from_partner(): return lax.ppermute(block, axis, route)  52 us
    ppermute x12, waiting for transfers between devices, from_partner(): return lax.ppermute(block, axis, route)  51.4 us
    all_to_all x1, blocking collectives, summed_on_arrival(): blocks = lax.all_to_all(split_up(value, dim, count), axis, 0, 0, tiled=True)  49.7 us
    all_to_all x1, waiting for transfers between devices, copy_for_each(): return lax.all_to_all(copies, axis, split_axis=0, concat_axis=0, tiled=True)  24.4 us
    all_gather x1, waiting for transfers between devices, on_device(): lax.all_gather(cotangent, 'ch', axis=1, tiled=True)  19.5 us
    ppermute x2, starting transfers between devices, extended(): lax.ppermute(head, axis, [((i + 1) % count, i) for i in range(ends)])  11 us
    all_to_all x1, starting transfers between devices, copy_for_each(): return lax.all_to_all(copies, axis, split_axis=0, concat_axis=0, tiled=True)  10 us
  transfers between devices with their start and end apart: 19, of which 14 were waited for; matrix products, arithmetic and copies ran while one was open for 5% of the time, Pallas kernels for 0%

commit v1 on v0

v1 whole, which is shorter than its diff:
```python
import functools

import jax
import jax.numpy as jnp
from jax import lax
from jax.experimental import pallas as pl
from jax.experimental.pallas import tpu as pltpu
from jax.sharding import PartitionSpec as P

BLOCK = 64
LOCAL = 2
CH = 128
TILE = 16
MESH = pl.DeviceIdType.MESH
F32 = jnp.float32
BF16 = jnp.bfloat16
root_two_pi = 0.7978845608028654


def mod(value, size):
    return lax.rem(value + size, size)


def both(first, second, axis):
    return jnp.concatenate([first, second], axis=axis)


def forward_factor(weights, state, mates):
    return [
        jnp.dot(w, both(own, mate, 0), preferred_element_type=F32).astype(BF16)
        for w, own, mate in zip(weights, state, mates)
    ]


def transposed_terms(weights, grads):
    return [
        lax.dot_general(w, g, (((0,), (0,)), ((), ())), preferred_element_type=F32)
        for w, g in zip(weights, grads)
    ]


def kernel(nb, zs, *refs):
    (
        inputs, taps_ref, mixing, pattern, w_in_hbm, w_out_hbm, cot,
        layer_out, conv_out, grad_out,
        x_v, mixl, win, wout,
        halo, ghalo, st0, sx, st1, sy, wx, wy,
        cot_all, mixed_all, hid, gact, act, ghid,
        rs_send, rs_recv, rs_own, ro_send, ro_recv, ro_own, term,
        g2, g1s, g1, g0s, g0, cross, out2,
        load_sem, halo_sem, cot_sem, wx_sem, wy_sem, sx_sem, sy_sem,
        cr_sem, mr_sem, rs_sem, ro_sem, gy_sem, gx_sem, lo_sem, gh_sem,
    ) = refs
    levels = nb.bit_length() - 1
    rows = nb * BLOCK
    far = zs // 2
    half = nb // 2
    count = nb * nb
    s = lax.axis_index("seq")
    z = lax.axis_index("ch")
    y = lax.div(s, nb)
    q = lax.rem(s, nb)
    up = mod(z + 1, zs)
    down = mod(z - 1, zs)

    loads = [
        pltpu.make_async_copy(inputs, x_v, load_sem.at[0]),
        pltpu.make_async_copy(mixing.at[pl.ds(0, LOCAL)], mixl, load_sem.at[1]),
        pltpu.make_async_copy(w_out_hbm, wout, load_sem.at[2]),
        pltpu.make_async_copy(w_in_hbm, win, load_sem.at[3]),
    ]
    for load in loads:
        load.start()

    barrier = pltpu.get_barrier_semaphore()

    def greet(seq, ch):
        pl.semaphore_signal(barrier, inc=1, device_id=(seq, ch), device_id_type=MESH)

    diagonal = jnp.where(y == q, 1, 0)
    @pl.when(s > 0)
    def _():
        greet(s - 1, z)

    @pl.when(s < count - 1)
    def _():
        greet(s + 1, z)

    for d in range(1, nb):
        greet(y * nb + mod(q + d, nb), z)
        greet(mod(y + d, nb) * nb + q, z)
    for j in range(nb):
        @pl.when(q * nb + j != s)
        def _():
            greet(q * nb + j, z)

        @pl.when(j * nb + y != s)
        def _():
            greet(j * nb + y, z)

    greet(s, up)
    greet(s, down)
    ends = jnp.where(s > 0, 1, 0) + jnp.where(s < count - 1, 1, 0)
    pl.semaphore_wait(barrier, 2 * (nb - 1) + 2 * (nb - diagonal) + 2 + ends)

    class Swap:
        def __init__(self, src, dst, sems, pick_src, pick_dst, slot, peer):
            self.src, self.dst, self.sems = src, dst, sems
            self.pick_src, self.pick_dst, self.slot, self.peer = pick_src, pick_dst, slot, peer

        def remote(self, t, into):
            return pltpu.make_async_remote_copy(
                src_ref=self.pick_src(self.src, t),
                dst_ref=self.pick_dst(self.dst, into),
                send_sem=self.sems.at[0, t],
                recv_sem=self.sems.at[1, into],
                device_id=(self.peer(t), z),
                device_id_type=MESH,
            )

        def own(self):
            return pltpu.make_async_copy(
                self.pick_src(self.src, self.slot), self.pick_dst(self.dst, self.slot), self.sems.at[1, self.slot]
            )

        def start(self):
            for d in range(1, nb):
                self.remote(mod(self.slot + d, nb), self.slot).start()
            self.own().start()

        def wait(self):
            self.own().wait()
            for d in range(1, nb):
                t = mod(self.slot + d, nb)
                self.remote(t, t).wait_recv()

        def drain(self):
            for d in range(1, nb):
                self.remote(mod(self.slot + d, nb), self.slot).wait_send()

    def first(ref, t):
        return ref.at[t]

    def over_q(src, dst, sems, pick_src=first, pick_dst=first):
        return Swap(src, dst, sems, pick_src, pick_dst, q, lambda t: y * nb + t)

    def over_y(src, dst, sems):
        return Swap(src, dst, sems, first, first, y, lambda t: t * nb + q)

    class Turn:
        def __init__(self, src, dst, sems, pick_src, pick_dst, slot, to):
            self.src, self.dst, self.sems = src, dst, sems
            self.pick_src, self.pick_dst, self.slot, self.to = pick_src, pick_dst, slot, to

        def remote(self, t, into):
            return pltpu.make_async_remote_copy(
                src_ref=self.pick_src(self.src, t),
                dst_ref=self.pick_dst(self.dst, into),
                send_sem=self.sems.at[0, t],
                recv_sem=self.sems.at[1, into],
                device_id=(self.to(t), z),
                device_id_type=MESH,
            )

        def own(self, t):
            return pltpu.make_async_copy(
                self.pick_src(self.src, t), self.pick_dst(self.dst, self.slot), self.sems.at[1, self.slot]
            )

        def start(self):
            for t in range(nb):
                @pl.when(self.to(t) != s)
                def _():
                    self.remote(t, self.slot).start()

                @pl.when(self.to(t) == s)
                def _():
                    self.own(t).start()

        def wait(self):
            for t in range(nb):
                mine = jnp.logical_and(y == q, self.slot == t)

                @pl.when(mine)
                def _():
                    self.own(t).wait()

                @pl.when(jnp.logical_not(mine))
                def _():
                    self.remote(t, t).wait_recv()

        def drain(self):
            for t in range(nb):
                @pl.when(self.to(t) != s)
                def _():
                    self.remote(t, self.slot).wait_send()

    class Gather:
        def __init__(self, buf, sems):
            self.buf, self.sems = buf, sems

        def copy(self, way, step, h, chunk):
            part = self.buf.at[chunk, pl.ds(h * half, half)]
            return pltpu.make_async_remote_copy(
                src_ref=part,
                dst_ref=part,
                send_sem=self.sems.at[0, way, step, h],
                recv_sem=self.sems.at[1, way, step, h],
                device_id=(s, up if way == 0 else down),
                device_id_type=MESH,
            )

        def halves(self, step):
            for h in range(2):
                for way in range(2):
                    if step < far - 1 or h == way:
                        yield way, h

        def chunk(self, way, step):
            return mod(z - step, zs) if way == 0 else mod(z + step, zs)

        def step(self, step):
            if step > 0:
                for h in range(2):
                    for way in range(2):
                        self.copy(way, step - 1, h, self.chunk(way, step)).wait_recv()
                        if step < far - 1 or h == way:
                            self.copy(way, step, h, self.chunk(way, step)).start()
            else:
                for way, h in self.halves(0):
                    self.copy(way, 0, h, z).start()

        def finish(self):
            for way, h in self.halves(far - 1):
                self.copy(way, far - 1, h, self.chunk(way, far)).wait_recv()

        def drain(self):
            for step in range(far):
                for way, h in self.halves(step):
                    self.copy(way, step, h, self.chunk(way, step)).wait_send()

    class Scatter:
        def __init__(self, send, recv, own, sems, pair):
            self.send, self.recv, self.own, self.sems, self.pair = send, recv, own, sems, pair

        def copy(self, way, step, h):
            return pltpu.make_async_remote_copy(
                src_ref=self.send.at[way, step, pl.ds(h * half, half)],
                dst_ref=self.recv.at[way, step, pl.ds(h * half, half)],
                send_sem=self.sems.at[0, way, step, h],
                recv_sem=self.sems.at[1, way, step, h],
                device_id=(s, up if way == 0 else down),
                device_id_type=MESH,
            )

        def arrived(self, way, step, h):
            if step < 0 or (step == 0 and h != way):
                return None
            self.copy(way, step, h).wait_recv()
            return self.recv[way, step, pl.ds(h * half, half)].astype(F32).reshape(half * BLOCK, CH)

        def stage(self, k):
            step = far - k
            near = z if k == far else mod(z - k, zs)
            term[...] = self.pair(mod(z + k, zs), near)
            for h in range(2):
                lines = pl.ds(h * half * BLOCK, half * BLOCK)
                if k == far:
                    value = term[lines, pl.ds(0, CH)]
                    self.send[h, step, pl.ds(h * half, half)] = value.astype(BF16).reshape(half, BLOCK, CH)
                    self.copy(h, step, h).start()
                    self.own[lines, :] = term[lines, pl.ds(CH, CH)]
                    continue
                for way in range(2):
                    value = term[lines, pl.ds(way * CH, CH)]
                    came = self.arrived(way, step - 1, h)
                    if came is not None:
                        value = value + came
                    self.send[way, step, pl.ds(h * half, half)] = value.astype(BF16).reshape(half, BLOCK, CH)
                    self.copy(way, step, h).start()

        def finish(self):
            totals = []
            for h in range(2):
                value = self.own[pl.ds(h * half * BLOCK, half * BLOCK), :]
                for way in range(2):
                    came = self.arrived(way, far - 1, h)
                    if came is not None:
                        value = value + came
                totals.append(value)
            return both(totals[0], totals[1], 0)

        def drain(self):
            for step in range(far):
                for h in range(2):
                    for way in range(2):
                        if step > 0 or h == way:
                            self.copy(way, step, h).wait_send()

    def rim(src_head, src_tail, dst, sems):
        return (
            pltpu.make_async_remote_copy(
                src_ref=src_tail, dst_ref=dst.at[0], send_sem=sems.at[0, 0], recv_sem=sems.at[1, 0],
                device_id=(s + 1, z), device_id_type=MESH,
            ),
            pltpu.make_async_remote_copy(
                src_ref=src_head, dst_ref=dst.at[1], send_sem=sems.at[0, 1], recv_sem=sems.at[1, 1],
                device_id=(s - 1, z), device_id_type=MESH,
            ),
        )

    def rim_start(pair, dst):
        @pl.when(s < count - 1)
        def _():
            pair[0].start()

        @pl.when(s > 0)
        def _():
            pair[1].start()

        @pl.when(s == 0)
        def _():
            dst[0] = jnp.zeros((TILE, CH), BF16)

        @pl.when(s == count - 1)
        def _():
            dst[1] = jnp.zeros((TILE, CH), BF16)

    def rim_wait(pair):
        @pl.when(s > 0)
        def _():
            pair[0].wait_recv()

        @pl.when(s < count - 1)
        def _():
            pair[1].wait_recv()

    def rim_drain(pair):
        @pl.when(s < count - 1)
        def _():
            pair[0].wait_send()

        @pl.when(s > 0)
        def _():
            pair[1].wait_send()

    def convolve(value, edges, before, same, after):
        value = value.astype(F32)
        line = lax.broadcasted_iota(jnp.int32, value.shape, 0)
        above = edges[0].astype(F32)[TILE - 1 : TILE, :]
        below = edges[1].astype(F32)[0:1, :]
        earlier = jnp.where(line == 0, above, pltpu.roll(value, 1, 0))
        later = jnp.where(line == rows - 1, below, pltpu.roll(value, rows - 1, 0))
        return (before * earlier + same * value + after * later).astype(BF16)

    def put(ref, blocks):
        for i, block in enumerate(blocks):
            ref[i] = block

    def forward_levels(weights, state):
        for level in range(levels):
            state = forward_factor(
                [weights[level, i] for i in range(nb)], state, [state[i ^ (1 << level)] for i in range(nb)]
            )
        return state

    def backward_levels(weights, grads):
        for level in reversed(range(levels)):
            terms = transposed_terms([weights[level, i] for i in range(nb)], grads)
            grads = [
                (terms[i][:BLOCK] + terms[i ^ (1 << level)][BLOCK:]).astype(BF16) for i in range(nb)
            ]
        return grads

    edges = rim(inputs.at[pl.ds(0, TILE)], inputs.at[pl.ds(rows - TILE, TILE)], halo, halo_sem)
    rim_start(edges, halo)
    cot_turn = Turn(
        cot, cot_all, cot_sem,
        lambda ref, t: ref.at[pl.ds(t * BLOCK, BLOCK)],
        lambda ref, t: ref.at[z, t], y, lambda t: q * nb + t,
    )
    cot_turn.start()
    wx_swap = over_q(
        mixing, wx, wx_sem,
        lambda ref, t: ref.at[pl.ds(LOCAL, levels), t],
        lambda ref, t: ref.at[pl.ds(0, levels), t],
    )
    wx_swap.start()
    wy_turn = Turn(
        mixing, wy, wy_sem,
        lambda ref, t: ref.at[pl.ds(LOCAL + levels, levels), t],
        lambda ref, t: ref.at[pl.ds(0, levels), t], y, lambda t: q * nb + t,
    )

    taps = taps_ref[...].astype(F32)
    tap0, tap1, tap2 = taps[0:1], taps[1:2], taps[2:3]
    loads[0].wait()
    rim_wait(edges)
    convolved = convolve(x_v[...], (halo[0], halo[1]), tap0, tap1, tap2)
    conv_out[...] = convolved
    st0[...] = convolved.reshape(nb, BLOCK, CH)
    loads[1].wait()
    for factor in range(LOCAL):
        state = [st0[i] for i in range(nb)]
        mates = [st0[pattern[factor, i]] for i in range(nb)]
        put(st0, forward_factor([mixl[factor, i] for i in range(nb)], state, mates))

    sx_swap = over_q(st0, sx, sx_sem)
    sx_swap.start()
    wy_turn.start()
    cot_turn.wait()
    cot_ring = Gather(cot_all, cr_sem)
    cot_ring.step(0)
    wx_swap.wait()
    sx_swap.wait()
    put(st1, forward_levels(wx, [sx[i] for i in range(nb)]))

    sy_swap = over_y(st1, sy, sy_sem)
    sy_swap.start()
    cot_ring.step(1) if far > 1 else None
    wy_turn.wait()
    sy_swap.wait()
    mixed = forward_levels(wy, [sy[i] for i in range(nb)])
    for i in range(nb):
        mixed_all[z, i] = mixed[i]
    mixed_ring = Gather(mixed_all, mr_sem)
    mixed_ring.step(0)

    def chunks(buf, first_chunk, second_chunk):
        return both(buf[first_chunk].reshape(rows, CH), buf[second_chunk].reshape(rows, CH), 1)

    def channels(index):
        return pl.ds(pl.multiple_of(index * CH, CH), CH)

    def add_grad_act(a, b, start):
        value = lax.dot_general(
            chunks(cot_all, a, b), both(wout[:, channels(a)], wout[:, channels(b)], 1),
            (((1,), (1,)), ((), ())), preferred_element_type=F32,
        )
        gact[...] = value if start else gact[...] + value

    def add_hidden(a, b, start):
        value = jnp.dot(
            chunks(mixed_all, a, b), both(win[channels(a), :], win[channels(b), :], 0),
            preferred_element_type=F32,
        )
        hid[...] = value if start else hid[...] + value

    loads[2].wait()
    loads[3].wait()
    for step in range(1, far):
        if step > 1:
            cot_ring.step(step)
        add_grad_act(mod(z - step, zs), mod(z + step, zs), step == 1)
        mixed_ring.step(step)
        add_hidden(mod(z - step, zs), mod(z + step, zs), step == 1)
    cot_ring.finish()
    add_grad_act(z, mod(z + far, zs), far == 1)
    mixed_ring.finish()
    add_hidden(z, mod(z + far, zs), far == 1)

    @pl.loop(0, nb)
    def _(i):
        lines = pl.ds(pl.multiple_of(i * BLOCK, BLOCK), BLOCK)
        v = hid[lines, :]
        square = v * v
        tanh_val = jnp.tanh(root_two_pi * (v + 0.044715 * square * v))
        plus = 0.5 * (1.0 + tanh_val)
        act[lines, :] = (v * plus).astype(BF16)
        slope = root_two_pi * (1.0 + 3.0 * 0.044715 * square)
        slope = plus + 0.5 * v * (1.0 - tanh_val * tanh_val) * slope
        ghid[lines, :] = (gact[lines, :] * slope).astype(BF16)

    def grad_pair(a, b):
        return lax.dot_general(
            ghid[...], both(win[channels(a), :], win[channels(b), :], 0),
            (((1,), (1,)), ((), ())), preferred_element_type=F32,
        )

    def out_pair(a, b):
        return jnp.dot(
            act[...], both(wout[:, channels(a)], wout[:, channels(b)], 1), preferred_element_type=F32
        )

    grad_sum = Scatter(rs_send, rs_recv, rs_own, rs_sem, grad_pair)
    out_sum = Scatter(ro_send, ro_recv, ro_own, ro_sem, out_pair)
    for k in range(far, 0, -1):
        grad_sum.stage(k)
    out_sum.stage(far)
    total = grad_sum.finish()
    grad_mixed = (cot_all[z].astype(F32).reshape(rows, CH) + total).astype(BF16).reshape(nb, BLOCK, CH)

    put(g2, backward_levels(wy, [grad_mixed[i] for i in range(nb)]))
    gy_swap = over_y(g2, g1, gy_sem)
    gy_swap.start()
    rest = list(range(far - 1, 0, -1))
    for k in rest[:2]:
        out_sum.stage(k)
    gy_swap.wait()
    put(g1s, backward_levels(wx, [g1[i] for i in range(nb)]))
    gx_swap = over_q(g1s, g0, gx_sem)
    gx_swap.start()
    for k in rest[2:]:
        out_sum.stage(k)
    gx_swap.wait()
    grads = [g0[i] for i in range(nb)]
    for factor in reversed(range(LOCAL)):
        terms = transposed_terms([mixl[factor, i] for i in range(nb)], grads)
        put(cross, [t[BLOCK:] for t in terms])
        grads = [(terms[i][:BLOCK] + cross[pattern[factor, i]]).astype(BF16) for i in range(nb)]
    put(g0s, grads)
    gedges = rim(
        g0s.at[0, pl.ds(0, TILE)], g0s.at[nb - 1, pl.ds(BLOCK - TILE, TILE)], ghalo, gh_sem
    )
    rim_start(gedges, ghalo)
    branch = out_sum.finish()
    put_mixed = (mixed_all[z].astype(F32).reshape(rows, CH) + branch).astype(BF16)
    out2[...] = put_mixed.reshape(nb, BLOCK, CH)
    lo_turn = Turn(
        out2, layer_out, lo_sem, first,
        lambda ref, t: ref.at[pl.ds(t * BLOCK, BLOCK)], q, lambda t: t * nb + y,
    )
    lo_turn.start()
    rim_wait(gedges)
    grad_out[...] = convolve(g0s[...].reshape(rows, CH), (ghalo[0], ghalo[1]), tap2, tap1, tap0)
    lo_turn.wait()

    rim_drain(edges)
    rim_drain(gedges)
    for transfer in (
        cot_turn, wx_swap, wy_turn, sx_swap, sy_swap, cot_ring, mixed_ring,
        grad_sum, out_sum, gy_swap, gx_swap, lo_turn,
    ):
        transfer.drain()


def on_device(nb, zs, inputs, conv_weight, mixing, pattern, w_in, w_out, cotangent):
    rows, _ = inputs.shape
    levels = nb.bit_length() - 1
    hidden = w_in.shape[1]
    channels = w_in.shape[0]
    far = zs // 2
    vmem = pltpu.VMEM
    dma = pltpu.SemaphoreType.DMA
    blocks = (nb, BLOCK, CH)
    scratch = [
        vmem((rows, CH), BF16),
        vmem((LOCAL, *blocks), BF16),
        vmem((channels, hidden), BF16),
        vmem((hidden, channels), BF16),
        vmem((2, TILE, CH), BF16),
        vmem((2, TILE, CH), BF16),
        *[vmem(blocks, BF16)] * 4,
        *[vmem((levels, *blocks), BF16)] * 2,
        *[vmem((zs, *blocks), BF16)] * 2,
        *[vmem((rows, hidden), F32)] * 2,
        *[vmem((rows, hidden), BF16)] * 2,
        *[vmem((2, far, *blocks), BF16)] * 2,
        vmem((rows, CH), F32),
        *[vmem((2, far, *blocks), BF16)] * 2,
        vmem((rows, CH), F32),
        vmem((rows, 2 * CH), F32),
        *[vmem(blocks, BF16)] * 5,
        vmem(blocks, F32),
        vmem(blocks, BF16),
        dma((4,)),
        dma((2, 2)),
        *[dma((2, nb))] * 5,
        *[dma((2, 2, far, 2))] * 4,
        *[dma((2, nb))] * 3,
        dma((2, 2)),
    ]
    out = jax.ShapeDtypeStruct((rows, CH), BF16)
    hbm = pl.BlockSpec(memory_space=pl.ANY)
    local = pl.BlockSpec(memory_space=pltpu.VMEM)
    return pl.pallas_call(
        functools.partial(kernel, nb, zs),
        out_shape=(out, out, out),
        in_specs=[hbm, local, hbm, pl.BlockSpec(memory_space=pltpu.SMEM), hbm, hbm, hbm],
        out_specs=(local, local, local),
        scratch_shapes=scratch,
        compiler_params=pltpu.CompilerParams(
            collective_id=0, has_side_effects=True, vmem_limit_bytes=56 * 1024 * 1024
        ),
    )(inputs, conv_weight, mixing, pattern, w_in, w_out, cotangent)


def solution(mesh):
    seq, zs = mesh.shape["seq"], mesh.shape["ch"]
    nb = 1 << ((seq.bit_length() - 1) // 2)
    return jax.shard_map(
        functools.partial(on_device, nb, zs),
        mesh=mesh,
        in_specs=(
            P("seq", "ch"),
            P(None, "ch"),
            P(None, "seq", None, None),
            P(None, "seq"),
            P(None, "ch"),
            P("ch", None),
            P("seq", "ch"),
        ),
        out_specs=(P("seq", "ch"), P("seq", "ch"), P("seq", "ch")),
        check_vma=False,
    )
```

time: 272 us -> 119 us (0.44)
  Pallas kernels: 0 us -> 114 us
  waiting for transfers between devices: 96 us -> 0 us
  starting transfers between devices: 78.3 us -> 0 us
  blocking collectives: 49.7 us -> 0 us
  matrix products: 18.9 us -> 0 us
  between operations: 14.8 us -> 0.65 us
  other arithmetic: 5.17 us -> 0 us
  local copies, waits for them, and re-layouts: 5.94 us -> 3.21 us
    pallas_call x0 -> x1, Pallas kernels: none -> 114 us  [on_device(): pl.pallas_call(functools.partial(kernel, nb, zs), out_shape=(out, out, ou...]
    ppermute x16 -> x0, starting transfers between devices: 68.2 us -> none  [the longest x12 52 us: from_partner(): return lax.ppermute(block, axis, route)]
    ppermute x16 -> x0, waiting for transfers between devices: 51.4 us -> none  [the longest x12 51.4 us: from_partner(): return lax.ppermute(block, axis, route)]
    all_to_all x1 -> x0, blocking collectives: 49.7 us -> none  [summed_on_arrival(): blocks = lax.all_to_all(split_up(value, dim, count), axis, 0, 0, tiled=True)]
    all_to_all x1 -> x0, waiting for transfers between devices: 24.4 us -> none  [copy_for_each(): return lax.all_to_all(copies, axis, split_axis=0, concat_axis=0, tiled=True)]
    all_gather x1 -> x0, waiting for transfers between devices: 19.5 us -> none  [on_device(): lax.all_gather(cotangent, 'ch', axis=1, tiled=True)]
    dot_general x35 -> x0, matrix products: 18.9 us -> none  [the longest x8 4.21 us: on_device(): jnp.einsum('bji,bjd->bid', weights[:, :, BLOCK:], grads, preferred_elemen...]
    all_to_all x1 -> x0, starting transfers between devices: 10 us -> none  [copy_for_each(): return lax.all_to_all(copies, axis, split_axis=0, concat_axis=0, tiled=True)]
  transfers between devices with their start and end apart: 19 -> 0, of which waited for: 14 -> 0; matrix products, arithmetic and copies ran while one was open for 5% -> 0% of each run, Pallas kernels for 0% -> 0%
where the time goes in v1:
time: 119 us; the launch traced here: 117 us
  Pallas kernels  114 us (96%)
  local copies, waits for them, and re-layouts  3.21 us (3%)
    pallas_call x1, Pallas kernels, on_device(): pl.pallas_call(functools.partial(kernel, nb, zs), out_shape=(out, out, ou...  114 us
    unnamed x7, local copies, waits for them, and re-layouts  3.21 us

profile of v1, /device:TPU:1, one launch (start us, length us, event | category | flops | bytes accessed | tf_op | source)
XLA Modules:
  0.0 117.4 jit_solution(8476770953671240733)
XLA Ops:
  0.6 113.5 %shard_map.94 = (bf16[512,128]{1,0:T(8,128)(2,1)}, bf16[512,128]{1,0:T(8,128)(2,1)}, bf16[512,128]{1,0:T(8,128)(2,1)}) custom-call(bf16[512,128]{1,0:T(8,128)(2,1)} %refs_0_.1, bf16[3,128]{1,0:T(4,128)(2,1)} %refs_1_.1, bf16[8,8,64,128]{3,2,1,0:T(8,128)(2,1)} %refs_2_.1, s32[2,8]{1,0:T(2,128)} %refs_3_.1, bf16[1024,512]{1,0:T(8,128)(2,1)} %refs_4_.1, ...), custom_call_target="tpu_custom_call" | custom-call | tf_op jit(solution)/shard_map/pallas_call | solution.py:576
  114.1 0.0 copy-start.1
  114.2 1.6 %copy.13 = bf16[512,128]{1,0:T(8,128)(2,1)} copy(bf16[512,128]{1,0:T(8,128)(2,1)} %get-tuple-element.6) | data formatting | bytes 262144
  115.8 0.0 copy-done.1
  115.8 0.0 copy-start
  115.8 0.7 copy.14
  116.4 0.3 copy-done
  116.7 0.7 copy.15
Async XLA Ops:
  114.1 1.6 %copy-start.1 = (bf16[512,128]{1,0:T(8,128)(2,1)S(1)}, bf16[512,128]{1,0:T(8,128)(2,1)}, u32[]{:S(2)}) copy-start(bf16[512,128]{1,0:T(8,128)(2,1)} %get-tuple-element.7) | copy-start | bytes 393220
  115.8 1.0 copy-start

commit v2 on v1

--- a/solution.py
+++ b/solution.py
@@ -11,6 +11,7 @@
 LOCAL = 2
 CH = 128
 TILE = 16
+SPLIT = BLOCK // TILE
 MESH = pl.DeviceIdType.MESH
 F32 = jnp.float32
 BF16 = jnp.bfloat16
@@ -41,20 +42,23 @@
 
 def kernel(nb, zs, *refs):
     (
-        inputs, taps_ref, mixing, pattern, w_in_hbm, w_out_hbm, cot,
+        inputs, taps_hbm, mixing, pattern_hbm, w_in_hbm, w_out_hbm, cot,
         layer_out, conv_out, grad_out,
-        x_v, mixl, win, wout,
-        halo, ghalo, st0, sx, st1, sy, wx, wy,
-        cot_all, mixed_all, hid, gact, act, ghid,
+        x_v, cv, taps_ref, pattern, mixl, win, wout,
+        halo, ghalo, st0, sx, st1, sy, wx, wy, wq,
+        cot_all, mixed_all, hid, ga0, ga1, ga2, act, ghid,
         rs_send, rs_recv, rs_own, ro_send, ro_recv, ro_own, term,
-        g2, g1s, g1, g0s, g0, cross, out2,
-        load_sem, halo_sem, cot_sem, wx_sem, wy_sem, sx_sem, sy_sem,
-        cr_sem, mr_sem, rs_sem, ro_sem, gy_sem, gx_sem, lo_sem, gh_sem,
+        g2, g1s, g1, g0s, g0, cross, out2, cs1, cs2, go_v,
+        load_sem, save_sem, halo_sem, wx_sem, wq_sem, wr_sem, wz_sem, sx_sem, sy_sem,
+        cr_sem, mr_sem, rs_sem, ro_sem, ax_sem, ay_sem, cx_sem, cy_sem,
+        gy_sem, gx_sem, lo_sem, gh_sem,
     ) = refs
     levels = nb.bit_length() - 1
     rows = nb * BLOCK
     far = zs // 2
-    half = nb // 2
+    parts = min(4, nb)
+    size = nb // parts
+    lines_of = size * BLOCK
     count = nb * nb
     s = lax.axis_index("seq")
     z = lax.axis_index("ch")
@@ -62,12 +66,18 @@
     q = lax.rem(s, nb)
     up = mod(z + 1, zs)
     down = mod(z - 1, zs)
+    up2 = mod(z + 2, zs)
+    down2 = mod(z - 2, zs)
+    quarter = lax.rem(z, SPLIT)
+    strip = pl.ds(pl.multiple_of(quarter * TILE, TILE), TILE)
 
     loads = [
         pltpu.make_async_copy(inputs, x_v, load_sem.at[0]),
         pltpu.make_async_copy(mixing.at[pl.ds(0, LOCAL)], mixl, load_sem.at[1]),
         pltpu.make_async_copy(w_out_hbm, wout, load_sem.at[2]),
         pltpu.make_async_copy(w_in_hbm, win, load_sem.at[3]),
+        pltpu.make_async_copy(taps_hbm, taps_ref, load_sem.at[4]),
+        pltpu.make_async_copy(pattern_hbm, pattern, load_sem.at[5]),
     ]
     for load in loads:
         load.start()
@@ -77,7 +87,6 @@
     def greet(seq, ch):
         pl.semaphore_signal(barrier, inc=1, device_id=(seq, ch), device_id_type=MESH)
 
-    diagonal = jnp.where(y == q, 1, 0)
     @pl.when(s > 0)
     def _():
         greet(s - 1, z)
@@ -89,19 +98,12 @@
     for d in range(1, nb):
         greet(y * nb + mod(q + d, nb), z)
         greet(mod(y + d, nb) * nb + q, z)
-    for j in range(nb):
-        @pl.when(q * nb + j != s)
-        def _():
-            greet(q * nb + j, z)
-
-        @pl.when(j * nb + y != s)
-        def _():
-            greet(j * nb + y, z)
-
     greet(s, up)
     greet(s, down)
+    greet(s, up2)
+    greet(s, down2)
     ends = jnp.where(s > 0, 1, 0) + jnp.where(s < count - 1, 1, 0)
-    pl.semaphore_wait(barrier, 2 * (nb - 1) + 2 * (nb - diagonal) + 2 + ends)
+    pl.semaphore_wait(barrier, 2 * (nb - 1) + 4 + ends)
 
     class Swap:
         def __init__(self, src, dst, sems, pick_src, pick_dst, slot, peer):
@@ -144,8 +146,8 @@
     def over_q(src, dst, sems, pick_src=first, pick_dst=first):
         return Swap(src, dst, sems, pick_src, pick_dst, q, lambda t: y * nb + t)
 
-    def over_y(src, dst, sems):
-        return Swap(src, dst, sems, first, first, y, lambda t: t * nb + q)
+    def over_y(src, dst, sems, pick_src=first, pick_dst=first):
+        return Swap(src, dst, sems, pick_src, pick_dst, y, lambda t: t * nb + q)
 
     class Turn:
         def __init__(self, src, dst, sems, pick_src, pick_dst, slot, to):
@@ -195,107 +197,148 @@
                 def _():
                     self.remote(t, self.slot).wait_send()
 
+    def ours(way, p):
+        return (p < parts // 2) == (way == 0)
+
     class Gather:
-        def __init__(self, buf, sems):
-            self.buf, self.sems = buf, sems
-
-        def copy(self, way, step, h, chunk):
-            part = self.buf.at[chunk, pl.ds(h * half, half)]
+        def __init__(self, pick, first_pick, sems):
+            self.pick, self.first_pick, self.sems = pick, first_pick, sems
+
+        def copy(self, way, step, p, chunk):
+            part = self.pick(chunk, p)
+            return pltpu.make_async_remote_copy(
+                src_ref=self.first_pick(p) if step == 0 else part,
+                dst_ref=part,
+                send_sem=self.sems.at[0, way, step, p],
+                recv_sem=self.sems.at[1, way, step, p],
+                device_id=(s, up if way == 0 else down),
+                device_id_type=MESH,
+            )
+
+        def chunk(self, way, step):
+            return mod(z - step, zs) if way == 0 else mod(z + step, zs)
+
+        def each(self, step):
+            for p in range(parts):
+                for way in range(2):
+                    if step < far - 1 or ours(way, p):
+                        yield way, p
+
+        def came(self, way, step, p):
+            part = self.pick(self.chunk(way, step + 1), p)
             return pltpu.make_async_remote_copy(
                 src_ref=part,
                 dst_ref=part,
-                send_sem=self.sems.at[0, way, step, h],
-                recv_sem=self.sems.at[1, way, step, h],
+                send_sem=self.sems.at[0, way, step, p],
+                recv_sem=self.sems.at[1, way, step, p],
                 device_id=(s, up if way == 0 else down),
                 device_id_type=MESH,
             )
 
-        def halves(self, step):
-            for h in range(2):
+        def step(self, step):
+            for p in range(parts):
                 for way in range(2):
-                    if step < far - 1 or h == way:
-                        yield way, h
-
-        def chunk(self, way, step):
-            return mod(z - step, zs) if way == 0 else mod(z + step, zs)
-
-        def step(self, step):
-            if step > 0:
-                for h in range(2):
-                    for way in range(2):
-                        self.copy(way, step - 1, h, self.chunk(way, step)).wait_recv()
-                        if step < far - 1 or h == way:
-                            self.copy(way, step, h, self.chunk(way, step)).start()
-            else:
-                for way, h in self.halves(0):
-                    self.copy(way, 0, h, z).start()
+                    if step > 0:
+                        self.came(way, step - 1, p).wait_recv()
+                    if step < far - 1 or ours(way, p):
+                        self.copy(way, step, p, self.chunk(way, step)).start()
 
         def finish(self):
-            for way, h in self.halves(far - 1):
-                self.copy(way, far - 1, h, self.chunk(way, far)).wait_recv()
+            for way, p in self.each(far - 1):
+                self.came(way, far - 1, p).wait_recv()
 
         def drain(self):
             for step in range(far):
-                for way, h in self.halves(step):
-                    self.copy(way, step, h, self.chunk(way, step)).wait_send()
+                for way, p in self.each(step):
+                    self.copy(way, step, p, self.chunk(way, step)).wait_send()
 
     class Scatter:
         def __init__(self, send, recv, own, sems, pair):
             self.send, self.recv, self.own, self.sems, self.pair = send, recv, own, sems, pair
 
-        def copy(self, way, step, h):
+        def copy(self, way, step, p):
             return pltpu.make_async_remote_copy(
-                src_ref=self.send.at[way, step, pl.ds(h * half, half)],
-                dst_ref=self.recv.at[way, step, pl.ds(h * half, half)],
-                send_sem=self.sems.at[0, way, step, h],
-                recv_sem=self.sems.at[1, way, step, h],
+                src_ref=self.send.at[way, step, pl.ds(p * size, size)],
+                dst_ref=self.recv.at[way, step, pl.ds(p * size, size)],
+                send_sem=self.sems.at[0, way, step, p],
+                recv_sem=self.sems.at[1, way, step, p],
                 device_id=(s, up if way == 0 else down),
                 device_id_type=MESH,
             )
 
-        def arrived(self, way, step, h):
-            if step < 0 or (step == 0 and h != way):
+        def arrived(self, way, step, p):
+            if step < 0 or (step == 0 and not ours(way, p)):
                 return None
-            self.copy(way, step, h).wait_recv()
-            return self.recv[way, step, pl.ds(h * half, half)].astype(F32).reshape(half * BLOCK, CH)
+            self.copy(way, step, p).wait_recv()
+            return self.recv[way, step, pl.ds(p * size, size)].astype(F32).reshape(lines_of, CH)
 
         def stage(self, k):
             step = far - k
             near = z if k == far else mod(z - k, zs)
             term[...] = self.pair(mod(z + k, zs), near)
-            for h in range(2):
-                lines = pl.ds(h * half * BLOCK, half * BLOCK)
-                if k == far:
-                    value = term[lines, pl.ds(0, CH)]
-                    self.send[h, step, pl.ds(h * half, half)] = value.astype(BF16).reshape(half, BLOCK, CH)
-                    self.copy(h, step, h).start()
-                    self.own[lines, :] = term[lines, pl.ds(CH, CH)]
-                    continue
+            for p in range(parts):
+                lines = pl.ds(p * lines_of, lines_of)
                 for way in range(2):
-                    value = term[lines, pl.ds(way * CH, CH)]
-                    came = self.arrived(way, step - 1, h)
-                    if came is not None:
-                        value = value + came
-                    self.send[way, step, pl.ds(h * half, half)] = value.astype(BF16).reshape(half, BLOCK, CH)
-                    self.copy(way, step, h).start()
+                    if k == far:
+                        if not ours(way, p):
+                            continue
+                        value = term[lines, pl.ds(0, CH)]
+                    else:
+                        value = term[lines, pl.ds(way * CH, CH)]
+                        came = self.arrived(way, step - 1, p)
+                        if came is not None:
+                            value = value + came
+                    self.send[way, step, pl.ds(p * size, size)] = value.astype(BF16).reshape(size, BLOCK, CH)
+                    self.copy(way, step, p).start()
+            if k == far:
+                self.own[...] = term[:, pl.ds(CH, CH)]
 
         def finish(self):
             totals = []
-            for h in range(2):
-                value = self.own[pl.ds(h * half * BLOCK, half * BLOCK), :]
+            for p in range(parts):
+                value = self.own[pl.ds(p * lines_of, lines_of), :]
                 for way in range(2):
-                    came = self.arrived(way, far - 1, h)
+                    came = self.arrived(way, far - 1, p)
                     if came is not None:
                         value = value + came
                 totals.append(value)
-            return both(totals[0], totals[1], 0)
+            return jnp.concatenate(totals, axis=0)
 
         def drain(self):
             for step in range(far):
-                for h in range(2):
+                for p in range(parts):
                     for way in range(2):
-                        if step > 0 or h == way:
-                            self.copy(way, step, h).wait_send()
+                        if step > 0 or ours(way, p):
+                            self.copy(way, step, p).wait_send()
+
+    class Spread:
+        def __init__(self):
+            hb = nb // 2
+            self.cases = [
+                (up, down, 1, pl.ds(0, nb)), (down, up, -1, pl.ds(0, nb)),
+                (up2, down2, 2, pl.ds(0, hb)), (down2, up2, -2, pl.ds(hb, hb)),
+            ]
+
+        def copy(self, case, theirs):
+            to, _, shift, slots = self.cases[case]
+            index = lax.rem(quarter - shift + 2 * SPLIT, SPLIT) if theirs else quarter
+            part = wy.at[pl.ds(0, levels), slots, pl.ds(pl.multiple_of(index * TILE, TILE), TILE)]
+            return pltpu.make_async_remote_copy(
+                src_ref=part, dst_ref=part, send_sem=wz_sem.at[0, case], recv_sem=wz_sem.at[1, case],
+                device_id=(s, to), device_id_type=MESH,
+            )
+
+        def start(self):
+            for case in range(4):
+                self.copy(case, False).start()
+
+        def wait(self):
+            for case in range(4):
+                self.copy(case, True).wait_recv()
+
+        def drain(self):
+            for case in range(4):
+                self.copy(case, False).wait_send()
 
     def rim(src_head, src_tail, dst, sems):
         return (
@@ -374,32 +417,37 @@
 
     edges = rim(inputs.at[pl.ds(0, TILE)], inputs.at[pl.ds(rows - TILE, TILE)], halo, halo_sem)
     rim_start(edges, halo)
-    cot_turn = Turn(
-        cot, cot_all, cot_sem,
-        lambda ref, t: ref.at[pl.ds(t * BLOCK, BLOCK)],
-        lambda ref, t: ref.at[z, t], y, lambda t: q * nb + t,
-    )
-    cot_turn.start()
+    cot_ring = Gather(
+        lambda chunk, p: cot_all.at[chunk, pl.ds(p * lines_of, lines_of)],
+        lambda p: cot.at[pl.ds(p * lines_of, lines_of)], cr_sem,
+    )
+    cot_ring.step(0)
+    own_cot = pltpu.make_async_copy(cot, cot_all.at[z], load_sem.at[6])
+    own_cot.start()
+    wq_swap = over_q(
+        mixing, wq, wq_sem,
+        lambda ref, t: ref.at[pl.ds(LOCAL + levels, levels), t, strip],
+        lambda ref, t: ref.at[pl.ds(0, levels), t],
+    )
+    wq_swap.start()
     wx_swap = over_q(
         mixing, wx, wx_sem,
         lambda ref, t: ref.at[pl.ds(LOCAL, levels), t],
         lambda ref, t: ref.at[pl.ds(0, levels), t],
     )
     wx_swap.start()
-    wy_turn = Turn(
-        mixing, wy, wy_sem,
-        lambda ref, t: ref.at[pl.ds(LOCAL + levels, levels), t],
-        lambda ref, t: ref.at[pl.ds(0, levels), t], y, lambda t: q * nb + t,
-    )
-
+
+    loads[4].wait()
     taps = taps_ref[...].astype(F32)
     tap0, tap1, tap2 = taps[0:1], taps[1:2], taps[2:3]
     loads[0].wait()
     rim_wait(edges)
-    convolved = convolve(x_v[...], (halo[0], halo[1]), tap0, tap1, tap2)
-    conv_out[...] = convolved
-    st0[...] = convolved.reshape(nb, BLOCK, CH)
+    cv[...] = convolve(x_v[...], (halo[0], halo[1]), tap0, tap1, tap2)
+    conv_save = pltpu.make_async_copy(cv, conv_out, save_sem.at[0])
+    conv_save.start()
+    st0[...] = cv[...].reshape(nb, BLOCK, CH)
     loads[1].wait()
+    loads[5].wait()
     for factor in range(LOCAL):
         state = [st0[i] for i in range(nb)]
         mates = [st0[pattern[factor, i]] for i in range(nb)]
@@ -407,57 +455,79 @@
 
     sx_swap = over_q(st0, sx, sx_sem)
     sx_swap.start()
-    wy_turn.start()
-    cot_turn.wait()
-    cot_ring = Gather(cot_all, cr_sem)
-    cot_ring.step(0)
+    if far > 1:
+        cot_ring.step(1)
+    wq_swap.wait()
+    wr_swap = over_y(
+        wq, wy, wr_sem,
+        lambda ref, t: ref.at[pl.ds(0, levels), t],
+        lambda ref, t: ref.at[pl.ds(0, levels), t, strip],
+    )
+    wr_swap.start()
+    if far > 2:
+        cot_ring.step(2)
     wx_swap.wait()
     sx_swap.wait()
     put(st1, forward_levels(wx, [sx[i] for i in range(nb)]))
 
     sy_swap = over_y(st1, sy, sy_sem)
     sy_swap.start()
-    cot_ring.step(1) if far > 1 else None
-    wy_turn.wait()
+    for step in range(3, far):
+        cot_ring.step(step)
+    wr_swap.wait()
+    spread = Spread()
+    spread.start()
+
+    def channels(index):
+        return pl.ds(pl.multiple_of(index * CH, CH), CH)
+
+    cot_ring.finish()
+    own_cot.wait()
+    loads[2].wait()
+    value = None
+    for c in range(0, zs, 2):
+        part = lax.dot_general(
+            both(cot_all[c], cot_all[c + 1], 1), wout[:, pl.ds(c * CH, 2 * CH)],
+            (((1,), (1,)), ((), ())), preferred_element_type=F32,
+        )
+        value = part if value is None else value + part
+    ga0[...] = value.astype(BF16).reshape(ga0.shape)
+    ax_swap = over_q(ga0, ga1, ax_sem)
+    ax_swap.start()
+    cx_swap = over_q(cot, cs1, cx_sem, lambda ref, t: ref.at[pl.ds(t * BLOCK, BLOCK)])
+    cx_swap.start()
     sy_swap.wait()
+    spread.wait()
     mixed = forward_levels(wy, [sy[i] for i in range(nb)])
     for i in range(nb):
         mixed_all[z, i] = mixed[i]
-    mixed_ring = Gather(mixed_all, mr_sem)
+    mixed_ring = Gather(
+        lambda chunk, p: mixed_all.at[chunk, pl.ds(p * size, size)],
+        lambda p: mixed_all.at[z, pl.ds(p * size, size)], mr_sem,
+    )
     mixed_ring.step(0)
-
-    def chunks(buf, first_chunk, second_chunk):
-        return both(buf[first_chunk].reshape(rows, CH), buf[second_chunk].reshape(rows, CH), 1)
-
-    def channels(index):
-        return pl.ds(pl.multiple_of(index * CH, CH), CH)
-
-    def add_grad_act(a, b, start):
-        value = lax.dot_general(
-            chunks(cot_all, a, b), both(wout[:, channels(a)], wout[:, channels(b)], 1),
-            (((1,), (1,)), ((), ())), preferred_element_type=F32,
-        )
-        gact[...] = value if start else gact[...] + value
 
     def add_hidden(a, b, start):
         value = jnp.dot(
-            chunks(mixed_all, a, b), both(win[channels(a), :], win[channels(b), :], 0),
+            both(mixed_all[a].reshape(rows, CH), mixed_all[b].reshape(rows, CH), 1),
+            both(win[channels(a), :], win[channels(b), :], 0),
             preferred_element_type=F32,
         )
         hid[...] = value if start else hid[...] + value
 
-    loads[2].wait()
+    ax_swap.wait()
+    ay_swap = over_y(ga1, ga2, ay_sem)
+    ay_swap.start()
+    cx_swap.wait()
+    cy_swap = over_y(cs1, cs2, cy_sem)
+    cy_swap.start()
     loads[3].wait()
     for step in range(1, far):
-        if step > 1:
-            cot_ring.step(step)
-        add_grad_act(mod(z - step, zs), mod(z + step, zs), step == 1)
         mixed_ring.step(step)
         add_hidden(mod(z - step, zs), mod(z + step, zs), step == 1)
-    cot_ring.finish()
-    add_grad_act(z, mod(z + far, zs), far == 1)
     mixed_ring.finish()
     add_hidden(z, mod(z + far, zs), far == 1)
+    ay_swap.wait()
 
     @pl.loop(0, nb)
     def _(i):
@@ -469,7 +539,7 @@
         act[lines, :] = (v * plus).astype(BF16)
         slope = root_two_pi * (1.0 + 3.0 * 0.044715 * square)
         slope = plus + 0.5 * v * (1.0 - tanh_val * tanh_val) * slope
-        ghid[lines, :] = (gact[lines, :] * slope).astype(BF16)
+        ghid[lines, :] = (ga2[i].astype(F32) * slope).astype(BF16)
 
     def grad_pair(a, b):
         return lax.dot_general(
@@ -487,8 +557,9 @@
     for k in range(far, 0, -1):
         grad_sum.stage(k)
     out_sum.stage(far)
+    cy_swap.wait()
     total = grad_sum.finish()
-    grad_mixed = (cot_all[z].astype(F32).reshape(rows, CH) + total).astype(BF16).reshape(nb, BLOCK, CH)
+    grad_mixed = (cs2[...].astype(F32).reshape(rows, CH) + total).astype(BF16).reshape(nb, BLOCK, CH)
 
     put(g2, backward_levels(wy, [grad_mixed[i] for i in range(nb)]))
     gy_swap = over_y(g2, g1, gy_sem)
@@ -514,24 +585,28 @@
     )
     rim_start(gedges, ghalo)
     branch = out_sum.finish()
-    put_mixed = (mixed_all[z].astype(F32).reshape(rows, CH) + branch).astype(BF16)
-    out2[...] = put_mixed.reshape(nb, BLOCK, CH)
+    whole = (mixed_all[z].astype(F32).reshape(rows, CH) + branch).astype(BF16)
+    out2[...] = whole.reshape(nb, BLOCK, CH)
     lo_turn = Turn(
         out2, layer_out, lo_sem, first,
         lambda ref, t: ref.at[pl.ds(t * BLOCK, BLOCK)], q, lambda t: t * nb + y,
     )
     lo_turn.start()
     rim_wait(gedges)
-    grad_out[...] = convolve(g0s[...].reshape(rows, CH), (ghalo[0], ghalo[1]), tap2, tap1, tap0)
-    lo_turn.wait()
+    go_v[...] = convolve(g0s[...].reshape(rows, CH), (ghalo[0], ghalo[1]), tap2, tap1, tap0)
+    grad_save = pltpu.make_async_copy(go_v, grad_out, save_sem.at[1])
+    grad_save.start()
 
     rim_drain(edges)
     rim_drain(gedges)
     for transfer in (
-        cot_turn, wx_swap, wy_turn, sx_swap, sy_swap, cot_ring, mixed_ring,
-        grad_sum, out_sum, gy_swap, gx_swap, lo_turn,
+        wq_swap, wx_swap, wr_swap, spread, sx_swap, sy_swap, ax_swap, ay_swap, cx_swap, cy_swap,
+        cot_ring, mixed_ring, grad_sum, out_sum, gy_swap, gx_swap, lo_turn,
     ):
         transfer.drain()
+    conv_save.wait()
+    lo_turn.wait()
+    grad_save.wait()
 
 
 def on_device(nb, zs, inputs, conv_weight, mixing, pattern, w_in, w_out, cotangent):
@@ -543,8 +618,13 @@
     vmem = pltpu.VMEM
     dma = pltpu.SemaphoreType.DMA
     blocks = (nb, BLOCK, CH)
+    parts = min(4, nb)
+    deep = (nb, BLOCK, hidden)
     scratch = [
         vmem((rows, CH), BF16),
+        vmem((rows, CH), BF16),
+        vmem(conv_weight.shape, BF16),
+        pltpu.SMEM(pattern.shape, jnp.int32),
         vmem((LOCAL, *blocks), BF16),
         vmem((channels, hidden), BF16),
         vmem((hidden, channels), BF16),
@@ -552,8 +632,11 @@
         vmem((2, TILE, CH), BF16),
         *[vmem(blocks, BF16)] * 4,
         *[vmem((levels, *blocks), BF16)] * 2,
-        *[vmem((zs, *blocks), BF16)] * 2,
-        *[vmem((rows, hidden), F32)] * 2,
+        vmem((levels, nb, TILE, CH), BF16),
+        vmem((zs, rows, CH), BF16),
+        vmem((zs, *blocks), BF16),
+        vmem((rows, hidden), F32),
+        *[vmem(deep, BF16)] * 3,
         *[vmem((rows, hidden), BF16)] * 2,
         *[vmem((2, far, *blocks), BF16)] * 2,
         vmem((rows, CH), F32),
@@ -562,22 +645,25 @@
         vmem((rows, 2 * CH), F32),
         *[vmem(blocks, BF16)] * 5,
         vmem(blocks, F32),
-        vmem(blocks, BF16),
-        dma((4,)),
+        *[vmem(blocks, BF16)] * 3,
+        vmem((rows, CH), BF16),
+        dma((7,)),
+        dma((2,)),
         dma((2, 2)),
-        *[dma((2, nb))] * 5,
-        *[dma((2, 2, far, 2))] * 4,
         *[dma((2, nb))] * 3,
+        dma((2, 4)),
+        *[dma((2, nb))] * 2,
+        *[dma((2, 2, far, parts))] * 4,
+        *[dma((2, nb))] * 7,
         dma((2, 2)),
     ]
     out = jax.ShapeDtypeStruct((rows, CH), BF16)
     hbm = pl.BlockSpec(memory_space=pl.ANY)
-    local = pl.BlockSpec(memory_space=pltpu.VMEM)
     return pl.pallas_call(
         functools.partial(kernel, nb, zs),
         out_shape=(out, out, out),
-        in_specs=[hbm, local, hbm, pl.BlockSpec(memory_space=pltpu.SMEM), hbm, hbm, hbm],
-        out_specs=(local, local, local),
+        in_specs=[hbm] * 7,
+        out_specs=(hbm, hbm, hbm),
         scratch_shapes=scratch,
         compiler_params=pltpu.CompilerParams(
             collective_id=0, has_side_effects=True, vmem_limit_bytes=56 * 1024 * 1024

time: 119 us -> 97.3 us (0.82)
  Pallas kernels: 114 us -> 92.5 us
    pallas_call x1, Pallas kernels: 114 us -> 92.5 us  [on_device(): pl.pallas_call(functools.partial(kernel, nb, zs), out_shape=(out, out, ou...]
where the time goes in v2:
time: 97.3 us; the launch traced here: 96.4 us
  Pallas kernels  92.5 us (95%)
  local copies, waits for them, and re-layouts  3.21 us (3%)
    pallas_call x1, Pallas kernels, on_device(): pl.pallas_call(functools.partial(kernel, nb, zs), out_shape=(out, out, ou...  92.5 us
    unnamed x7, local copies, waits for them, and re-layouts  3.21 us

profile of v2, /device:TPU:1, one launch (start us, length us, event | category | flops | bytes accessed | tf_op | source)
XLA Modules:
  0.0 96.4 jit_solution(17911372585823925314)
XLA Ops:
  0.6 92.5 %shard_map.94 = (bf16[512,128]{1,0:T(8,128)(2,1)}, bf16[512,128]{1,0:T(8,128)(2,1)}, bf16[512,128]{1,0:T(8,128)(2,1)}) custom-call(bf16[512,128]{1,0:T(8,128)(2,1)} %refs_0_.1, bf16[3,128]{1,0:T(4,128)(2,1)} %refs_1_.1, bf16[8,8,64,128]{3,2,1,0:T(8,128)(2,1)} %refs_2_.1, s32[2,8]{1,0:T(2,128)} %refs_3_.1, bf16[1024,512]{1,0:T(8,128)(2,1)} %refs_4_.1, ...), custom_call_target="tpu_custom_call" | custom-call | tf_op jit(solution)/shard_map/pallas_call | solution.py:662
  93.2 0.0 copy-start.1
  93.2 1.6 %copy.13 = bf16[512,128]{1,0:T(8,128)(2,1)} copy(bf16[512,128]{1,0:T(8,128)(2,1)} %get-tuple-element.6) | data formatting | bytes 262144
  94.8 0.0 copy-done.1
  94.8 0.0 copy-start
  94.8 0.7 copy.14
  95.4 0.3 copy-done
  95.7 0.7 copy.15
Async XLA Ops:
  93.2 1.6 %copy-start.1 = (bf16[512,128]{1,0:T(8,128)(2,1)S(1)}, bf16[512,128]{1,0:T(8,128)(2,1)}, u32[]{:S(2)}) copy-start(bf16[512,128]{1,0:T(8,128)(2,1)} %get-tuple-element.7) | copy-start | bytes 393220
  94.8 1.0 copy-start

commit v3 on v2

--- a/solution.py
+++ b/solution.py
@@ -12,6 +12,7 @@
 CH = 128
 TILE = 16
 SPLIT = BLOCK // TILE
+TOP = BLOCK - TILE
 MESH = pl.DeviceIdType.MESH
 F32 = jnp.float32
 BF16 = jnp.bfloat16
@@ -46,11 +47,11 @@
         layer_out, conv_out, grad_out,
         x_v, cv, taps_ref, pattern, mixl, win, wout,
         halo, ghalo, st0, sx, st1, sy, wx, wy, wq,
-        cot_all, mixed_all, hid, ga0, ga1, ga2, act, ghid,
+        cot_all, cb1, cb_all, gb, mixed_all, hid, ga0, ga1, ga2, act, ghid,
         rs_send, rs_recv, rs_own, ro_send, ro_recv, ro_own, term,
         g2, g1s, g1, g0s, g0, cross, out2, cs1, cs2, go_v,
         load_sem, save_sem, halo_sem, wx_sem, wq_sem, wr_sem, wz_sem, sx_sem, sy_sem,
-        cr_sem, mr_sem, rs_sem, ro_sem, ax_sem, ay_sem, cx_sem, cy_sem,
+        bx_sem, by_sem, br_sem, ring_sem, cr_sem, mr_sem, rs_sem, ro_sem, ax_sem, ay_sem, cx_sem, cy_sem,
         gy_sem, gx_sem, lo_sem, gh_sem,
     ) = refs
     levels = nb.bit_length() - 1
@@ -105,24 +106,31 @@
     ends = jnp.where(s > 0, 1, 0) + jnp.where(s < count - 1, 1, 0)
     pl.semaphore_wait(barrier, 2 * (nb - 1) + 4 + ends)
 
+    def arrival(view, sem):
+        pltpu.make_async_copy(view, view, sem).wait()
+
     class Swap:
-        def __init__(self, src, dst, sems, pick_src, pick_dst, slot, peer):
-            self.src, self.dst, self.sems = src, dst, sems
-            self.pick_src, self.pick_dst, self.slot, self.peer = pick_src, pick_dst, slot, peer
+        def __init__(self, src, dst, sems, slot, peer, pick_src=None, pick_dst=None, many_src=None, many_dst=None):
+            self.src, self.dst, self.sems, self.slot, self.peer = src, dst, sems, slot, peer
+            self.pick_src, self.pick_dst = pick_src or first, pick_dst or first
+            self.many_src, self.many_dst = many_src or several, many_dst or several
+
+        def recv_sem(self, t):
+            return self.sems.at[1]
 
         def remote(self, t, into):
             return pltpu.make_async_remote_copy(
                 src_ref=self.pick_src(self.src, t),
                 dst_ref=self.pick_dst(self.dst, into),
-                send_sem=self.sems.at[0, t],
-                recv_sem=self.sems.at[1, into],
+                send_sem=self.sems.at[0],
+                recv_sem=self.recv_sem(into),
                 device_id=(self.peer(t), z),
                 device_id_type=MESH,
             )
 
         def own(self):
             return pltpu.make_async_copy(
-                self.pick_src(self.src, self.slot), self.pick_dst(self.dst, self.slot), self.sems.at[1, self.slot]
+                self.pick_src(self.src, self.slot), self.pick_dst(self.dst, self.slot), self.recv_sem(self.slot)
             )
 
         def start(self):
@@ -131,86 +139,76 @@
             self.own().start()
 
         def wait(self):
-            self.own().wait()
-            for d in range(1, nb):
-                t = mod(self.slot + d, nb)
-                self.remote(t, t).wait_recv()
+            arrival(self.many_dst(self.dst, nb), self.sems.at[1])
 
         def drain(self):
-            for d in range(1, nb):
-                self.remote(mod(self.slot + d, nb), self.slot).wait_send()
+            arrival(self.many_src(self.src, nb - 1), self.sems.at[0])
+
+    class Stream(Swap):
+        def recv_sem(self, t):
+            return self.sems.at[1 + t]
+
+        def wait(self, t):
+            arrival(self.pick_dst(self.dst, t), self.recv_sem(t))
 
     def first(ref, t):
         return ref.at[t]
 
-    def over_q(src, dst, sems, pick_src=first, pick_dst=first):
-        return Swap(src, dst, sems, pick_src, pick_dst, q, lambda t: y * nb + t)
-
-    def over_y(src, dst, sems, pick_src=first, pick_dst=first):
-        return Swap(src, dst, sems, pick_src, pick_dst, y, lambda t: t * nb + q)
+    def several(ref, n):
+        return ref.at[pl.ds(0, n)]
+
+    def by_q(t):
+        return y * nb + t
+
+    def by_y(t):
+        return t * nb + q
 
     class Turn:
-        def __init__(self, src, dst, sems, pick_src, pick_dst, slot, to):
+        def __init__(self, src, dst, sems):
             self.src, self.dst, self.sems = src, dst, sems
-            self.pick_src, self.pick_dst, self.slot, self.to = pick_src, pick_dst, slot, to
-
-        def remote(self, t, into):
-            return pltpu.make_async_remote_copy(
-                src_ref=self.pick_src(self.src, t),
-                dst_ref=self.pick_dst(self.dst, into),
-                send_sem=self.sems.at[0, t],
-                recv_sem=self.sems.at[1, into],
-                device_id=(self.to(t), z),
-                device_id_type=MESH,
-            )
-
-        def own(self, t):
-            return pltpu.make_async_copy(
-                self.pick_src(self.src, t), self.pick_dst(self.dst, self.slot), self.sems.at[1, self.slot]
-            )
 
         def start(self):
             for t in range(nb):
-                @pl.when(self.to(t) != s)
+                into = self.dst.at[pl.ds(q * BLOCK, BLOCK)]
+
+                @pl.when(t * nb + y != s)
                 def _():
-                    self.remote(t, self.slot).start()
-
-                @pl.when(self.to(t) == s)
+                    pltpu.make_async_remote_copy(
+                        src_ref=self.src.at[t], dst_ref=into, send_sem=self.sems.at[0], recv_sem=self.sems.at[1],
+                        device_id=(t * nb + y, z), device_id_type=MESH,
+                    ).start()
+
+                @pl.when(t * nb + y == s)
                 def _():
-                    self.own(t).start()
+                    pltpu.make_async_copy(self.src.at[t], into, self.sems.at[1]).start()
 
         def wait(self):
-            for t in range(nb):
-                mine = jnp.logical_and(y == q, self.slot == t)
-
-                @pl.when(mine)
-                def _():
-                    self.own(t).wait()
-
-                @pl.when(jnp.logical_not(mine))
-                def _():
-                    self.remote(t, t).wait_recv()
+            arrival(self.dst, self.sems.at[1])
 
         def drain(self):
-            for t in range(nb):
-                @pl.when(self.to(t) != s)
-                def _():
-                    self.remote(t, self.slot).wait_send()
-
-    def ours(way, p):
-        return (p < parts // 2) == (way == 0)
+            @pl.when(y == q)
+            def _():
+                arrival(self.src.at[pl.ds(0, nb - 1)], self.sems.at[0])
+
+            @pl.when(y != q)
+            def _():
+                arrival(self.src, self.sems.at[0])
+
+    def ours(way, p, count=parts):
+        return (p < count // 2) == (way == 0)
 
     class Gather:
-        def __init__(self, pick, first_pick, sems):
-            self.pick, self.first_pick, self.sems = pick, first_pick, sems
+        def __init__(self, buf, parts, pick, first_pick, send_sem, sems):
+            self.parts = parts
+            self.buf, self.pick, self.first_pick, self.send_sem, self.sems = buf, pick, first_pick, send_sem, sems
 
         def copy(self, way, step, p, chunk):
             part = self.pick(chunk, p)
             return pltpu.make_async_remote_copy(
                 src_ref=self.first_pick(p) if step == 0 else part,
                 dst_ref=part,
-                send_sem=self.sems.at[0, way, step, p],
-                recv_sem=self.sems.at[1, way, step, p],
+                send_sem=self.send_sem.at[0],
+                recv_sem=self.sems.at[way, step, p],
                 device_id=(s, up if way == 0 else down),
                 device_id_type=MESH,
             )
@@ -219,9 +217,9 @@
             return mod(z - step, zs) if way == 0 else mod(z + step, zs)
 
         def each(self, step):
-            for p in range(parts):
+            for p in range(self.parts):
                 for way in range(2):
-                    if step < far - 1 or ours(way, p):
+                    if step < far - 1 or ours(way, p, self.parts):
                         yield way, p
 
         def came(self, way, step, p):
@@ -229,18 +227,18 @@
             return pltpu.make_async_remote_copy(
                 src_ref=part,
                 dst_ref=part,
-                send_sem=self.sems.at[0, way, step, p],
-                recv_sem=self.sems.at[1, way, step, p],
+                send_sem=self.send_sem.at[0],
+                recv_sem=self.sems.at[way, step, p],
                 device_id=(s, up if way == 0 else down),
                 device_id_type=MESH,
             )
 
         def step(self, step):
-            for p in range(parts):
+            for p in range(self.parts):
                 for way in range(2):
                     if step > 0:
                         self.came(way, step - 1, p).wait_recv()
-                    if step < far - 1 or ours(way, p):
+                    if step < far - 1 or ours(way, p, self.parts):
                         self.copy(way, step, p, self.chunk(way, step)).start()
 
         def finish(self):
@@ -248,20 +246,23 @@
                 self.came(way, far - 1, p).wait_recv()
 
         def drain(self):
-            for step in range(far):
-                for way, p in self.each(step):
-                    self.copy(way, step, p, self.chunk(way, step)).wait_send()
+            arrival(self.buf.at[pl.ds(0, zs - 1)], self.send_sem.at[0])
 
     class Scatter:
-        def __init__(self, send, recv, own, sems, pair):
-            self.send, self.recv, self.own, self.sems, self.pair = send, recv, own, sems, pair
+        def __init__(self, send, recv, own, send_sem, sems, pair):
+            self.send, self.recv, self.own, self.send_sem, self.sems, self.pair = send, recv, own, send_sem, sems, pair
+
+        def at(self, way, step, p):
+            slot = zs - 2 if step == 0 else 2 * (step - 1) + way
+            return slot, pl.ds(p * size, size)
 
         def copy(self, way, step, p):
+            slot, blocks = self.at(way, step, p)
             return pltpu.make_async_remote_copy(
-                src_ref=self.send.at[way, step, pl.ds(p * size, size)],
-                dst_ref=self.recv.at[way, step, pl.ds(p * size, size)],
-                send_sem=self.sems.at[0, way, step, p],
-                recv_sem=self.sems.at[1, way, step, p],
+                src_ref=self.send.at[slot, blocks],
+                dst_ref=self.recv.at[slot, blocks],
+                send_sem=self.send_sem.at[0],
+                recv_sem=self.sems.at[way, step, p],
                 device_id=(s, up if way == 0 else down),
                 device_id_type=MESH,
             )
@@ -270,26 +271,27 @@
             if step < 0 or (step == 0 and not ours(way, p)):
                 return None
             self.copy(way, step, p).wait_recv()
-            return self.recv[way, step, pl.ds(p * size, size)].astype(F32).reshape(lines_of, CH)
+            slot, blocks = self.at(way, step, p)
+            return self.recv[slot, blocks].astype(F32).reshape(lines_of, CH)
+
+        def pass_on(self, way, step, p, value):
+            slot, blocks = self.at(way, step, p)
+            self.send[slot, blocks] = value.astype(BF16).reshape(size, BLOCK, CH)
+            self.copy(way, step, p).start()
 
         def stage(self, k):
             step = far - k
             near = z if k == far else mod(z - k, zs)
             term[...] = self.pair(mod(z + k, zs), near)
-            for p in range(parts):
-                lines = pl.ds(p * lines_of, lines_of)
-                for way in range(2):
-                    if k == far:
-                        if not ours(way, p):
-                            continue
-                        value = term[lines, pl.ds(0, CH)]
-                    else:
-                        value = term[lines, pl.ds(way * CH, CH)]
-                        came = self.arrived(way, step - 1, p)
-                        if came is not None:
-                            value = value + came
-                    self.send[way, step, pl.ds(p * size, size)] = value.astype(BF16).reshape(size, BLOCK, CH)
-                    self.copy(way, step, p).start()
+            todo = [(way, p) for p in range(parts) for way in range(2)]
+            if k == far:
+                todo = [(way, p) for way, p in todo if ours(way, p)]
+            elif k == far - 1:
+                todo.sort(key=lambda item: ours(*item))
+            for way, p in todo:
+                value = term[pl.ds(p * lines_of, lines_of), pl.ds(0 if k == far else way * CH, CH)]
+                came = self.arrived(way, step - 1, p)
+                self.pass_on(way, step, p, value if came is None else value + came)
             if k == far:
                 self.own[...] = term[:, pl.ds(CH, CH)]
 
@@ -305,11 +307,7 @@
             return jnp.concatenate(totals, axis=0)
 
         def drain(self):
-            for step in range(far):
-                for p in range(parts):
-                    for way in range(2):
-                        if step > 0 or ours(way, p):
-                            self.copy(way, step, p).wait_send()
+            arrival(self.send, self.send_sem.at[0])
 
     class Spread:
         def __init__(self):
@@ -417,23 +415,27 @@
 
     edges = rim(inputs.at[pl.ds(0, TILE)], inputs.at[pl.ds(rows - TILE, TILE)], halo, halo_sem)
     rim_start(edges, halo)
+    upper, last = pl.ds(0, TOP), pl.ds(TOP, TILE)
     cot_ring = Gather(
-        lambda chunk, p: cot_all.at[chunk, pl.ds(p * lines_of, lines_of)],
-        lambda p: cot.at[pl.ds(p * lines_of, lines_of)], cr_sem,
+        cot_all, parts,
+        lambda chunk, p: cot_all.at[chunk, pl.ds(p * size, size)],
+        lambda p: cot.at[pl.ds(p * size, size), upper], ring_sem.at[pl.ds(0, 1)], cr_sem,
     )
     cot_ring.step(0)
-    own_cot = pltpu.make_async_copy(cot, cot_all.at[z], load_sem.at[6])
+    own_cot = pltpu.make_async_copy(cot.at[pl.ds(0, nb), upper], cot_all.at[z], load_sem.at[6])
     own_cot.start()
-    wq_swap = over_q(
-        mixing, wq, wq_sem,
-        lambda ref, t: ref.at[pl.ds(LOCAL + levels, levels), t, strip],
-        lambda ref, t: ref.at[pl.ds(0, levels), t],
+    low, high = pl.ds(LOCAL, levels), pl.ds(LOCAL + levels, levels)
+    every = pl.ds(0, levels)
+    wq_swap = Swap(
+        mixing, wq, wq_sem, q, by_q,
+        lambda ref, t: ref.at[high, t, strip], lambda ref, t: ref.at[every, t],
+        lambda ref, n: ref.at[high, pl.ds(0, n), strip], lambda ref, n: ref.at[every, pl.ds(0, n)],
     )
     wq_swap.start()
-    wx_swap = over_q(
-        mixing, wx, wx_sem,
-        lambda ref, t: ref.at[pl.ds(LOCAL, levels), t],
-        lambda ref, t: ref.at[pl.ds(0, levels), t],
+    wx_swap = Swap(
+        mixing, wx, wx_sem, q, by_q,
+        lambda ref, t: ref.at[low, t], lambda ref, t: ref.at[every, t],
+        lambda ref, n: ref.at[low, pl.ds(0, n)], lambda ref, n: ref.at[every, pl.ds(0, n)],
     )
     wx_swap.start()
 
@@ -453,15 +455,20 @@
         mates = [st0[pattern[factor, i]] for i in range(nb)]
         put(st0, forward_factor([mixl[factor, i] for i in range(nb)], state, mates))
 
-    sx_swap = over_q(st0, sx, sx_sem)
+    sx_swap = Swap(st0, sx, sx_sem, q, by_q)
     sx_swap.start()
+    bx_swap = Swap(
+        cot, cb1, bx_sem, q, by_q,
+        lambda ref, t: ref.at[t, last], None, lambda ref, n: ref.at[pl.ds(0, n), last],
+    )
+    bx_swap.start()
     if far > 1:
         cot_ring.step(1)
     wq_swap.wait()
-    wr_swap = over_y(
-        wq, wy, wr_sem,
-        lambda ref, t: ref.at[pl.ds(0, levels), t],
-        lambda ref, t: ref.at[pl.ds(0, levels), t, strip],
+    wr_swap = Swap(
+        wq, wy, wr_sem, y, by_y,
+        lambda ref, t: ref.at[every, t], lambda ref, t: ref.at[every, t, strip],
+        lambda ref, n: ref.at[every, pl.ds(0, n)], lambda ref, n: ref.at[every, pl.ds(0, n), strip],
     )
     wr_swap.start()
     if far > 2:
@@ -470,31 +477,43 @@
     sx_swap.wait()
     put(st1, forward_levels(wx, [sx[i] for i in range(nb)]))
 
-    sy_swap = over_y(st1, sy, sy_sem)
+    sy_swap = Swap(st1, sy, sy_sem, y, by_y)
     sy_swap.start()
-    for step in range(3, far):
-        cot_ring.step(step)
     wr_swap.wait()
     spread = Spread()
     spread.start()
+    bx_swap.wait()
+    by_swap = Swap(
+        cb1, cb_all, by_sem, y, by_y, None, lambda ref, t: ref.at[z, t], None, lambda ref, n: ref.at[z, pl.ds(0, n)]
+    )
+    by_swap.start()
+    for step in range(3, far):
+        cot_ring.step(step)
 
     def channels(index):
         return pl.ds(pl.multiple_of(index * CH, CH), CH)
+
+    def grad_act(buf):
+        value = None
+        lines = buf.shape[1] * buf.shape[2]
+        for c in range(0, zs, 2):
+            part = lax.dot_general(
+                both(buf[c].reshape(lines, CH), buf[c + 1].reshape(lines, CH), 1), wout[:, pl.ds(c * CH, 2 * CH)],
+                (((1,), (1,)), ((), ())), preferred_element_type=F32,
+            )
+            value = part if value is None else value + part
+        return value
 
     cot_ring.finish()
     own_cot.wait()
     loads[2].wait()
-    value = None
-    for c in range(0, zs, 2):
-        part = lax.dot_general(
-            both(cot_all[c], cot_all[c + 1], 1), wout[:, pl.ds(c * CH, 2 * CH)],
-            (((1,), (1,)), ((), ())), preferred_element_type=F32,
-        )
-        value = part if value is None else value + part
-    ga0[...] = value.astype(BF16).reshape(ga0.shape)
-    ax_swap = over_q(ga0, ga1, ax_sem)
+    ga0[...] = grad_act(cot_all).astype(BF16).reshape(ga0.shape)
+    ax_swap = Stream(ga0, ga1, ax_sem, q, by_q)
     ax_swap.start()
-    cx_swap = over_q(cot, cs1, cx_sem, lambda ref, t: ref.at[pl.ds(t * BLOCK, BLOCK)])
+    cx_swap = Swap(
+        cot, cs1, cx_sem, q, by_q,
+        lambda ref, t: ref.at[t, upper], None, lambda ref, n: ref.at[pl.ds(0, n), upper],
+    )
     cx_swap.start()
     sy_swap.wait()
     spread.wait()
@@ -502,10 +521,19 @@
     for i in range(nb):
         mixed_all[z, i] = mixed[i]
     mixed_ring = Gather(
+        mixed_all, parts,
         lambda chunk, p: mixed_all.at[chunk, pl.ds(p * size, size)],
-        lambda p: mixed_all.at[z, pl.ds(p * size, size)], mr_sem,
+        lambda p: mixed_all.at[z, pl.ds(p * size, size)], ring_sem.at[pl.ds(1, 1)], mr_sem,
     )
     mixed_ring.step(0)
+    by_swap.wait()
+    wide = nb // 2
+    last_ring = Gather(
+        cb_all, 2,
+        lambda chunk, p: cb_all.at[chunk, pl.ds(p * wide, wide)],
+        lambda p: cb_all.at[z, pl.ds(p * wide, wide)], ring_sem.at[pl.ds(4, 1)], br_sem,
+    )
+    last_ring.step(0)
 
     def add_hidden(a, b, start):
         value = jnp.dot(
@@ -515,16 +543,28 @@
         )
         hid[...] = value if start else hid[...] + value
 
-    ax_swap.wait()
-    ay_swap = over_y(ga1, ga2, ay_sem)
-    ay_swap.start()
-    cx_swap.wait()
-    cy_swap = over_y(cs1, cs2, cy_sem)
-    cy_swap.start()
+    ay_swap = Swap(ga1, ga2, ay_sem, y, by_y)
+    cy_swap = Swap(cs1, cs2, cy_sem, y, by_y)
     loads[3].wait()
+    for d in range(nb):
+        t = mod(q + d, nb)
+        ax_swap.wait(t)
+
+        @pl.when(t == y)
+        def _():
+            ay_swap.own().start()
+
+        @pl.when(t != y)
+        def _():
+            ay_swap.remote(t, y).start()
     for step in range(1, far):
         mixed_ring.step(step)
+        last_ring.step(step)
         add_hidden(mod(z - step, zs), mod(z + step, zs), step == 1)
+    cx_swap.wait()
+    cy_swap.start()
+    last_ring.finish()
+    gb[...] = grad_act(cb_all)
     mixed_ring.finish()
     add_hidden(z, mod(z + far, zs), far == 1)
     ay_swap.wait()
@@ -539,7 +579,9 @@
         act[lines, :] = (v * plus).astype(BF16)
         slope = root_two_pi * (1.0 + 3.0 * 0.044715 * square)
         slope = plus + 0.5 * v * (1.0 - tanh_val * tanh_val) * slope
-        ghid[lines, :] = (ga2[i].astype(F32) * slope).astype(BF16)
+        strip_of = pl.ds(pl.multiple_of(i * TILE, TILE), TILE)
+        slope_in = both(ga2[i].astype(F32), gb[strip_of, :], 0)
+        ghid[lines, :] = (slope_in * slope).astype(BF16)
 
     def grad_pair(a, b):
         return lax.dot_general(
@@ -552,27 +594,36 @@
             act[...], both(wout[:, channels(a)], wout[:, channels(b)], 1), preferred_element_type=F32
         )
 
-    grad_sum = Scatter(rs_send, rs_recv, rs_own, rs_sem, grad_pair)
-    out_sum = Scatter(ro_send, ro_recv, ro_own, ro_sem, out_pair)
-    for k in range(far, 0, -1):
+    grad_sum = Scatter(rs_send, rs_recv, rs_own, ring_sem.at[pl.ds(2, 1)], rs_sem, grad_pair)
+    out_sum = Scatter(ro_send, ro_recv, ro_own, ring_sem.at[pl.ds(3, 1)], ro_sem, out_pair)
+    for k in range(far, 1, -1):
         grad_sum.stage(k)
     out_sum.stage(far)
+    grad_sum.stage(1)
+    rest = list(range(far - 1, 0, -1))
+    for k in rest[:1]:
+        out_sum.stage(k)
     cy_swap.wait()
     total = grad_sum.finish()
-    grad_mixed = (cs2[...].astype(F32).reshape(rows, CH) + total).astype(BF16).reshape(nb, BLOCK, CH)
+    own_grad = both(cs2[...], cb_all[z], 1).astype(F32).reshape(rows, CH)
+    grad_mixed = (own_grad + total).astype(BF16).reshape(nb, BLOCK, CH)
 
     put(g2, backward_levels(wy, [grad_mixed[i] for i in range(nb)]))
-    gy_swap = over_y(g2, g1, gy_sem)
+    gy_swap = Swap(g2, g1, gy_sem, y, by_y)
     gy_swap.start()
-    rest = list(range(far - 1, 0, -1))
-    for k in rest[:2]:
+    for k in rest[1:2]:
         out_sum.stage(k)
     gy_swap.wait()
     put(g1s, backward_levels(wx, [g1[i] for i in range(nb)]))
-    gx_swap = over_q(g1s, g0, gx_sem)
+    gx_swap = Swap(g1s, g0, gx_sem, q, by_q)
     gx_swap.start()
     for k in rest[2:]:
         out_sum.stage(k)
+    branch = out_sum.finish()
+    whole = (mixed_all[z].astype(F32).reshape(rows, CH) + branch).astype(BF16)
+    out2[...] = whole.reshape(nb, BLOCK, CH)
+    lo_turn = Turn(out2, layer_out, lo_sem)
+    lo_turn.start()
     gx_swap.wait()
     grads = [g0[i] for i in range(nb)]
     for factor in reversed(range(LOCAL)):
@@ -584,14 +635,6 @@
         g0s.at[0, pl.ds(0, TILE)], g0s.at[nb - 1, pl.ds(BLOCK - TILE, TILE)], ghalo, gh_sem
     )
     rim_start(gedges, ghalo)
-    branch = out_sum.finish()
-    whole = (mixed_all[z].astype(F32).reshape(rows, CH) + branch).astype(BF16)
-    out2[...] = whole.reshape(nb, BLOCK, CH)
-    lo_turn = Turn(
-        out2, layer_out, lo_sem, first,
-        lambda ref, t: ref.at[pl.ds(t * BLOCK, BLOCK)], q, lambda t: t * nb + y,
-    )
-    lo_turn.start()
     rim_wait(gedges)
     go_v[...] = convolve(g0s[...].reshape(rows, CH), (ghalo[0], ghalo[1]), tap2, tap1, tap0)
     grad_save = pltpu.make_async_copy(go_v, grad_out, save_sem.at[1])
@@ -600,13 +643,22 @@
     rim_drain(edges)
     rim_drain(gedges)
     for transfer in (
-        wq_swap, wx_swap, wr_swap, spread, sx_swap, sy_swap, ax_swap, ay_swap, cx_swap, cy_swap,
-        cot_ring, mixed_ring, grad_sum, out_sum, gy_swap, gx_swap, lo_turn,
+        wq_swap, wx_swap, wr_swap, spread, sx_swap, sy_swap, ax_swap, ay_swap, cx_swap, cy_swap, bx_swap, by_swap,
+        cot_ring, last_ring, mixed_ring, grad_sum, out_sum, gy_swap, gx_swap, lo_turn,
     ):
         transfer.drain()
     conv_save.wait()
     lo_turn.wait()
     grad_save.wait()
+
+
+def publish(*refs):
+    sources, targets, sem = refs[:3], refs[3:6], refs[6]
+    copies = [pltpu.make_async_copy(a, b, sem.at[i]) for i, (a, b) in enumerate(zip(sources, targets))]
+    for copy in copies:
+        copy.start()
+    for copy in copies:
+        copy.wait()
 
 
 def on_device(nb, zs, inputs, conv_weight, mixing, pattern, w_in, w_out, cotangent):
@@ -619,7 +671,7 @@
     dma = pltpu.SemaphoreType.DMA
     blocks = (nb, BLOCK, CH)
     parts = min(4, nb)
-    deep = (nb, BLOCK, hidden)
+    deep = (nb, TOP, hidden)
     scratch = [
         vmem((rows, CH), BF16),
         vmem((rows, CH), BF16),
@@ -633,42 +685,59 @@
         *[vmem(blocks, BF16)] * 4,
         *[vmem((levels, *blocks), BF16)] * 2,
         vmem((levels, nb, TILE, CH), BF16),
-        vmem((zs, rows, CH), BF16),
+        vmem((zs, nb, TOP, CH), BF16),
+        vmem((nb, TILE, CH), BF16),
+        vmem((zs, nb, TILE, CH), BF16),
+        vmem((nb * TILE, hidden), F32),
         vmem((zs, *blocks), BF16),
         vmem((rows, hidden), F32),
         *[vmem(deep, BF16)] * 3,
         *[vmem((rows, hidden), BF16)] * 2,
-        *[vmem((2, far, *blocks), BF16)] * 2,
+        *[vmem((zs - 1, *blocks), BF16)] * 2,
         vmem((rows, CH), F32),
-        *[vmem((2, far, *blocks), BF16)] * 2,
+        *[vmem((zs - 1, *blocks), BF16)] * 2,
         vmem((rows, CH), F32),
         vmem((rows, 2 * CH), F32),
         *[vmem(blocks, BF16)] * 5,
         vmem(blocks, F32),
-        *[vmem(blocks, BF16)] * 3,
+        vmem(blocks, BF16),
+        *[vmem((nb, TOP, CH), BF16)] * 2,
         vmem((rows, CH), BF16),
         dma((7,)),
         dma((2,)),
         dma((2, 2)),
-        *[dma((2, nb))] * 3,
+        *[dma((2,))] * 3,
         dma((2, 4)),
-        *[dma((2, nb))] * 2,
-        *[dma((2, 2, far, parts))] * 4,
-        *[dma((2, nb))] * 7,
+        *[dma((2,))] * 4,
+        dma((2, far, 2)),
+        dma((5,)),
+        *[dma((2, far, parts))] * 4,
+        dma((1 + nb,)),
+        *[dma((2,))] * 6,
         dma((2, 2)),
     ]
     out = jax.ShapeDtypeStruct((rows, CH), BF16)
     hbm = pl.BlockSpec(memory_space=pl.ANY)
-    return pl.pallas_call(
+    results = pl.pallas_call(
         functools.partial(kernel, nb, zs),
         out_shape=(out, out, out),
         in_specs=[hbm] * 7,
         out_specs=(hbm, hbm, hbm),
         scratch_shapes=scratch,
         compiler_params=pltpu.CompilerParams(
-            collective_id=0, has_side_effects=True, vmem_limit_bytes=56 * 1024 * 1024
+            collective_id=0, has_side_effects=True, vmem_limit_bytes=24 * 1024 * 1024
         ),
-    )(inputs, conv_weight, mixing, pattern, w_in, w_out, cotangent)
+    )(*[pltpu.with_memory_space_constraint(v, pltpu.HBM) for v in (
+        inputs, conv_weight, mixing, pattern, w_in, w_out, cotangent.reshape(blocks)
+    )])
+    return pl.pallas_call(
+        publish,
+        out_shape=(out, out, out),
+        in_specs=[pl.BlockSpec(memory_space=pltpu.VMEM)] * 3,
+        out_specs=(hbm, hbm, hbm),
+        scratch_shapes=[dma((3,))],
+        compiler_params=pltpu.CompilerParams(vmem_limit_bytes=4 * 1024 * 1024),
+    )(*results)
 
 
 def solution(mesh):

time: 97.3 us -> 91.3 us (0.938)
  the two profiles are of different devices: /device:TPU:1 before, /device:TPU:4 now
where the time goes in v3:
time: 91.3 us; the launch traced here: 91.1 us
  Pallas kernels  90.5 us (99%)
    pallas_call x1, Pallas kernels, on_device(): pl.pallas_call(functools.partial(kernel, nb, zs), out_shape=(out, out, ou...  89.7 us

profile of v3, /device:TPU:4, one launch (start us, length us, event | category | flops | bytes accessed | tf_op | source)
XLA Modules:
  0.0 91.1 jit_solution(5774574761237178627)
XLA Ops:
  0.6 89.7 %shard_map.94 = (bf16[512,128]{1,0:T(8,128)(2,1)S(1)}, bf16[512,128]{1,0:T(8,128)(2,1)S(1)}, bf16[512,128]{1,0:T(8,128)(2,1)S(1)}) custom-call(bf16[512,128]{1,0:T(8,128)(2,1)} %refs_0_.1, bf16[3,128]{1,0:T(4,128)(2,1)} %refs_1_.1, bf16[8,8,64,128]{3,2,1,0:T(8,128)(2,1)} %refs_2_.1, s32[2,8]{1,0:T(2,128)} %refs_3_.1, bf16[1024,512]{1,0:T(8,128)(2,1)} %refs_4_.1, ...), custom_call_target="tpu_custom_call" | custom-call | tf_op jit(solution)/shard_map/pallas_call | solution.py:721
  90.4 0.8 shard_map.95

commit v4 on v3

--- a/solution.py
+++ b/solution.py
@@ -167,8 +167,8 @@
         def __init__(self, src, dst, sems):
             self.src, self.dst, self.sems = src, dst, sems
 
-        def start(self):
-            for t in range(nb):
+        def start(self, blocks):
+            for t in blocks:
                 into = self.dst.at[pl.ds(q * BLOCK, BLOCK)]
 
                 @pl.when(t * nb + y != s)
@@ -295,16 +295,16 @@
             if k == far:
                 self.own[...] = term[:, pl.ds(CH, CH)]
 
+        def total(self, p):
+            value = self.own[pl.ds(p * lines_of, lines_of), :]
+            for way in range(2):
+                came = self.arrived(way, far - 1, p)
+                if came is not None:
+                    value = value + came
+            return value
+
         def finish(self):
-            totals = []
-            for p in range(parts):
-                value = self.own[pl.ds(p * lines_of, lines_of), :]
-                for way in range(2):
-                    came = self.arrived(way, far - 1, p)
-                    if came is not None:
-                        value = value + came
-                totals.append(value)
-            return jnp.concatenate(totals, axis=0)
+            return jnp.concatenate([self.total(p) for p in range(parts)], axis=0)
 
         def drain(self):
             arrival(self.send, self.send_sem.at[0])
@@ -479,6 +479,8 @@
 
     sy_swap = Swap(st1, sy, sy_sem, y, by_y)
     sy_swap.start()
+    for step in range(3, far):
+        cot_ring.step(step)
     wr_swap.wait()
     spread = Spread()
     spread.start()
@@ -487,8 +489,6 @@
         cb1, cb_all, by_sem, y, by_y, None, lambda ref, t: ref.at[z, t], None, lambda ref, n: ref.at[z, pl.ds(0, n)]
     )
     by_swap.start()
-    for step in range(3, far):
-        cot_ring.step(step)
 
     def channels(index):
         return pl.ds(pl.multiple_of(index * CH, CH), CH)
@@ -546,21 +546,22 @@
     ay_swap = Swap(ga1, ga2, ay_sem, y, by_y)
     cy_swap = Swap(cs1, cs2, cy_sem, y, by_y)
     loads[3].wait()
-    for d in range(nb):
-        t = mod(q + d, nb)
-        ax_swap.wait(t)
-
-        @pl.when(t == y)
-        def _():
-            ay_swap.own().start()
-
-        @pl.when(t != y)
-        def _():
-            ay_swap.remote(t, y).start()
     for step in range(1, far):
         mixed_ring.step(step)
         last_ring.step(step)
         add_hidden(mod(z - step, zs), mod(z + step, zs), step == 1)
+        if step == 1:
+            for d in range(nb):
+                t = mod(q + d, nb)
+                ax_swap.wait(t)
+
+                @pl.when(t == y)
+                def _():
+                    ay_swap.own().start()
+
+                @pl.when(t != y)
+                def _():
+                    ay_swap.remote(t, y).start()
     cx_swap.wait()
     cy_swap.start()
     last_ring.finish()
@@ -613,17 +614,18 @@
     gy_swap.start()
     for k in rest[1:2]:
         out_sum.stage(k)
+    for k in rest[2:]:
+        out_sum.stage(k)
     gy_swap.wait()
     put(g1s, backward_levels(wx, [g1[i] for i in range(nb)]))
     gx_swap = Swap(g1s, g0, gx_sem, q, by_q)
     gx_swap.start()
-    for k in rest[2:]:
-        out_sum.stage(k)
-    branch = out_sum.finish()
-    whole = (mixed_all[z].astype(F32).reshape(rows, CH) + branch).astype(BF16)
-    out2[...] = whole.reshape(nb, BLOCK, CH)
     lo_turn = Turn(out2, layer_out, lo_sem)
-    lo_turn.start()
+    for p in range(parts):
+        blocks = pl.ds(p * size, size)
+        whole = mixed_all[z, blocks].astype(F32).reshape(lines_of, CH) + out_sum.total(p)
+        out2[blocks] = whole.astype(BF16).reshape(size, BLOCK, CH)
+        lo_turn.start(range(p * size, (p + 1) * size))
     gx_swap.wait()
     grads = [g0[i] for i in range(nb)]
     for factor in reversed(range(LOCAL)):

time: 91.3 us -> 86.3 us (0.945)
  the two profiles are of different devices: /device:TPU:4 before, /device:TPU:1 now
where the time goes in v4:
time: 86.3 us; the launch traced here: 85.9 us
  Pallas kernels  85.2 us (99%)
    pallas_call x1, Pallas kernels, on_device(): pl.pallas_call(functools.partial(kernel, nb, zs), out_shape=(out, out, ou...  84.5 us

profile of v4, /device:TPU:1, one launch (start us, length us, event | category | flops | bytes accessed | tf_op | source)
XLA Modules:
  0.0 85.9 jit_solution(7154932656370808223)
XLA Ops:
  0.6 84.5 %shard_map.94 = (bf16[512,128]{1,0:T(8,128)(2,1)S(1)}, bf16[512,128]{1,0:T(8,128)(2,1)S(1)}, bf16[512,128]{1,0:T(8,128)(2,1)S(1)}) custom-call(bf16[512,128]{1,0:T(8,128)(2,1)} %refs_0_.1, bf16[3,128]{1,0:T(4,128)(2,1)} %refs_1_.1, bf16[8,8,64,128]{3,2,1,0:T(8,128)(2,1)} %refs_2_.1, s32[2,8]{1,0:T(2,128)} %refs_3_.1, bf16[1024,512]{1,0:T(8,128)(2,1)} %refs_4_.1, ...), custom_call_target="tpu_custom_call" | custom-call | tf_op jit(solution)/shard_map/pallas_call | solution.py:723
  85.1 0.8 shard_map.95

commit v5 on v4

--- a/solution.py
+++ b/solution.py
@@ -48,10 +48,10 @@
         x_v, cv, taps_ref, pattern, mixl, win, wout,
         halo, ghalo, st0, sx, st1, sy, wx, wy, wq,
         cot_all, cb1, cb_all, gb, mixed_all, hid, ga0, ga1, ga2, act, ghid,
-        rs_send, rs_recv, rs_own, ro_send, ro_recv, ro_own, term,
+        rs_send, rs_recv, rs_own, ro_send, ro_recv, ro_own, term, grad_terms,
         g2, g1s, g1, g0s, g0, cross, out2, cs1, cs2, go_v,
         load_sem, save_sem, halo_sem, wx_sem, wq_sem, wr_sem, wz_sem, sx_sem, sy_sem,
-        bx_sem, by_sem, br_sem, ring_sem, cr_sem, mr_sem, rs_sem, ro_sem, ax_sem, ay_sem, cx_sem, cy_sem,
+        bx_sem, by_sem, br_sem, ring_sem, cr_sem, mr_sem, ax_sem, ay_sem, cx_sem, cy_sem,
         gy_sem, gx_sem, lo_sem, gh_sem,
     ) = refs
     levels = nb.bit_length() - 1
@@ -249,8 +249,17 @@
             arrival(self.buf.at[pl.ds(0, zs - 1)], self.send_sem.at[0])
 
     class Scatter:
-        def __init__(self, send, recv, own, send_sem, sems, pair):
+        def __init__(self, send, recv, own, send_sem, sems, pair, terms=None):
             self.send, self.recv, self.own, self.send_sem, self.sems, self.pair = send, recv, own, send_sem, sems, pair
+            self.ahead = terms is not None
+            self.terms = terms
+
+        def prepare(self, k):
+            near = z if k == far else mod(z - k, zs)
+            self.term(k)[...] = self.pair(mod(z + k, zs), near)
+
+        def term(self, k):
+            return self.terms.at[far - k] if self.ahead else term
 
         def at(self, way, step, p):
             slot = zs - 2 if step == 0 else 2 * (step - 1) + way
@@ -281,19 +290,25 @@
 
         def stage(self, k):
             step = far - k
-            near = z if k == far else mod(z - k, zs)
-            term[...] = self.pair(mod(z + k, zs), near)
+            value_of = self.term(k)
+            if k == far or not self.ahead:
+                self.prepare(k)
             todo = [(way, p) for p in range(parts) for way in range(2)]
             if k == far:
                 todo = [(way, p) for way, p in todo if ours(way, p)]
             elif k == far - 1:
                 todo.sort(key=lambda item: ours(*item))
-            for way, p in todo:
-                value = term[pl.ds(p * lines_of, lines_of), pl.ds(0 if k == far else way * CH, CH)]
+            for index, (way, p) in enumerate(todo):
+                if k == far - 1 and index == parts and self.ahead:
+                    for later in range(k - 1, 0, -1):
+                        self.prepare(later)
+                value = value_of[pl.ds(p * lines_of, lines_of), pl.ds(0 if k == far else way * CH, CH)]
                 came = self.arrived(way, step - 1, p)
                 self.pass_on(way, step, p, value if came is None else value + came)
             if k == far:
-                self.own[...] = term[:, pl.ds(CH, CH)]
+                self.own[...] = value_of[:, pl.ds(CH, CH)]
+                if self.ahead and far > 1:
+                    self.prepare(k - 1)
 
         def total(self, p):
             value = self.own[pl.ds(p * lines_of, lines_of), :]
@@ -595,8 +610,8 @@
             act[...], both(wout[:, channels(a)], wout[:, channels(b)], 1), preferred_element_type=F32
         )
 
-    grad_sum = Scatter(rs_send, rs_recv, rs_own, ring_sem.at[pl.ds(2, 1)], rs_sem, grad_pair)
-    out_sum = Scatter(ro_send, ro_recv, ro_own, ring_sem.at[pl.ds(3, 1)], ro_sem, out_pair)
+    grad_sum = Scatter(rs_send, rs_recv, rs_own, ring_sem.at[pl.ds(2, 1)], mr_sem, grad_pair, grad_terms)
+    out_sum = Scatter(ro_send, ro_recv, ro_own, ring_sem.at[pl.ds(3, 1)], cr_sem, out_pair)
     for k in range(far, 1, -1):
         grad_sum.stage(k)
     out_sum.stage(far)
@@ -700,6 +715,7 @@
         *[vmem((zs - 1, *blocks), BF16)] * 2,
         vmem((rows, CH), F32),
         vmem((rows, 2 * CH), F32),
+        vmem((far, rows, 2 * CH), F32),
         *[vmem(blocks, BF16)] * 5,
         vmem(blocks, F32),
         vmem(blocks, BF16),
@@ -713,7 +729,7 @@
         *[dma((2,))] * 4,
         dma((2, far, 2)),
         dma((5,)),
-        *[dma((2, far, parts))] * 4,
+        *[dma((2, far, parts))] * 2,
         dma((1 + nb,)),
         *[dma((2,))] * 6,
         dma((2, 2)),
@@ -727,7 +743,7 @@
         out_specs=(hbm, hbm, hbm),
         scratch_shapes=scratch,
         compiler_params=pltpu.CompilerParams(
-            collective_id=0, has_side_effects=True, vmem_limit_bytes=24 * 1024 * 1024
+            collective_id=0, has_side_effects=True, vmem_limit_bytes=28 * 1024 * 1024
         ),
     )(*[pltpu.with_memory_space_constraint(v, pltpu.HBM) for v in (
         inputs, conv_weight, mixing, pattern, w_in, w_out, cotangent.reshape(blocks)

time: 86.3 us -> 85.9 us (level)
  no operation moved by 1% of the time
where the time goes in v5:
time: 85.9 us; the launch traced here: 85.5 us
  Pallas kernels  84.9 us (99%)
    pallas_call x1, Pallas kernels, on_device(): pl.pallas_call(functools.partial(kernel, nb, zs), out_shape=(out, out, ou...  84.1 us

profile of v5, /device:TPU:1, one launch (start us, length us, event | category | flops | bytes accessed | tf_op | source)
XLA Modules:
  0.0 85.5 jit_solution(17027443720787383342)
XLA Ops:
  0.6 84.1 %shard_map.94 = (bf16[512,128]{1,0:T(8,128)(2,1)S(1)}, bf16[512,128]{1,0:T(8,128)(2,1)S(1)}, bf16[512,128]{1,0:T(8,128)(2,1)S(1)}) custom-call(bf16[512,128]{1,0:T(8,128)(2,1)} %refs_0_.1, bf16[3,128]{1,0:T(4,128)(2,1)} %refs_1_.1, bf16[8,8,64,128]{3,2,1,0:T(8,128)(2,1)} %refs_2_.1, s32[2,8]{1,0:T(2,128)} %refs_3_.1, bf16[1024,512]{1,0:T(8,128)(2,1)} %refs_4_.1, ...), custom_call_target="tpu_custom_call" | custom-call | tf_op jit(solution)/shard_map/pallas_call | solution.py:739
  84.7 0.8 shard_map.95

commit v6 on v5

--- a/solution.py
+++ b/solution.py
@@ -51,7 +51,7 @@
         rs_send, rs_recv, rs_own, ro_send, ro_recv, ro_own, term, grad_terms,
         g2, g1s, g1, g0s, g0, cross, out2, cs1, cs2, go_v,
         load_sem, save_sem, halo_sem, wx_sem, wq_sem, wr_sem, wz_sem, sx_sem, sy_sem,
-        bx_sem, by_sem, br_sem, ring_sem, cr_sem, mr_sem, ax_sem, ay_sem, cx_sem, cy_sem,
+        bx_sem, by_sem, ring_sem, cr_sem, mr_sem, ax_sem, ay_sem, cx_sem, cy_sem,
         gy_sem, gx_sem, lo_sem, gh_sem,
     ) = refs
     levels = nb.bit_length() - 1
@@ -332,26 +332,26 @@
                 (up2, down2, 2, pl.ds(0, hb)), (down2, up2, -2, pl.ds(hb, hb)),
             ]
 
-        def copy(self, case, theirs):
+        def copy(self, case, level, theirs):
             to, _, shift, slots = self.cases[case]
             index = lax.rem(quarter - shift + 2 * SPLIT, SPLIT) if theirs else quarter
-            part = wy.at[pl.ds(0, levels), slots, pl.ds(pl.multiple_of(index * TILE, TILE), TILE)]
+            part = wy.at[level, slots, pl.ds(pl.multiple_of(index * TILE, TILE), TILE)]
             return pltpu.make_async_remote_copy(
-                src_ref=part, dst_ref=part, send_sem=wz_sem.at[0, case], recv_sem=wz_sem.at[1, case],
+                src_ref=part, dst_ref=part, send_sem=wz_sem.at[0], recv_sem=wz_sem.at[1 + 4 * level + case],
                 device_id=(s, to), device_id_type=MESH,
             )
 
         def start(self):
+            for level in range(levels):
+                for case in range(4):
+                    self.copy(case, level, False).start()
+
+        def wait(self, level):
             for case in range(4):
-                self.copy(case, False).start()
-
-        def wait(self):
-            for case in range(4):
-                self.copy(case, True).wait_recv()
+                self.copy(case, level, True).wait_recv()
 
         def drain(self):
-            for case in range(4):
-                self.copy(case, False).wait_send()
+            arrival(wy.at[pl.ds(0, levels), pl.ds(0, nb), pl.ds(0, 3 * TILE)], wz_sem.at[0])
 
     def rim(src_head, src_tail, dst, sems):
         return (
@@ -413,8 +413,10 @@
         for i, block in enumerate(blocks):
             ref[i] = block
 
-    def forward_levels(weights, state):
+    def forward_levels(weights, state, before=None):
         for level in range(levels):
+            if before is not None:
+                before(level)
             state = forward_factor(
                 [weights[level, i] for i in range(nb)], state, [state[i ^ (1 << level)] for i in range(nb)]
             )
@@ -531,8 +533,15 @@
     )
     cx_swap.start()
     sy_swap.wait()
-    spread.wait()
-    mixed = forward_levels(wy, [sy[i] for i in range(nb)])
+    by_swap.wait()
+    wide = nb // 2
+    last_ring = Gather(
+        cb_all, 2,
+        lambda chunk, p: cb_all.at[chunk, pl.ds(p * wide, wide)],
+        lambda p: cb_all.at[z, pl.ds(p * wide, wide)], ring_sem.at[pl.ds(4, 1)], cr_sem,
+    )
+    last_ring.step(0)
+    mixed = forward_levels(wy, [sy[i] for i in range(nb)], spread.wait)
     for i in range(nb):
         mixed_all[z, i] = mixed[i]
     mixed_ring = Gather(
@@ -541,14 +550,6 @@
         lambda p: mixed_all.at[z, pl.ds(p * size, size)], ring_sem.at[pl.ds(1, 1)], mr_sem,
     )
     mixed_ring.step(0)
-    by_swap.wait()
-    wide = nb // 2
-    last_ring = Gather(
-        cb_all, 2,
-        lambda chunk, p: cb_all.at[chunk, pl.ds(p * wide, wide)],
-        lambda p: cb_all.at[z, pl.ds(p * wide, wide)], ring_sem.at[pl.ds(4, 1)], br_sem,
-    )
-    last_ring.step(0)
 
     def add_hidden(a, b, start):
         value = jnp.dot(
@@ -558,13 +559,17 @@
         )
         hid[...] = value if start else hid[...] + value
 
+    def one_hidden(a):
+        return jnp.dot(mixed_all[a].reshape(rows, CH), win[channels(a), :], preferred_element_type=F32)
+
     ay_swap = Swap(ga1, ga2, ay_sem, y, by_y)
     cy_swap = Swap(cs1, cs2, cy_sem, y, by_y)
     loads[3].wait()
+    hid[...] = one_hidden(z)
     for step in range(1, far):
+        last_ring.step(step)
         mixed_ring.step(step)
-        last_ring.step(step)
-        add_hidden(mod(z - step, zs), mod(z + step, zs), step == 1)
+        add_hidden(mod(z - step, zs), mod(z + step, zs), False)
         if step == 1:
             for d in range(nb):
                 t = mod(q + d, nb)
@@ -582,7 +587,7 @@
     last_ring.finish()
     gb[...] = grad_act(cb_all)
     mixed_ring.finish()
-    add_hidden(z, mod(z + far, zs), far == 1)
+    hid[...] += one_hidden(mod(z + far, zs))
     ay_swap.wait()
 
     @pl.loop(0, nb)
@@ -725,9 +730,8 @@
         dma((2,)),
         dma((2, 2)),
         *[dma((2,))] * 3,
-        dma((2, 4)),
+        dma((1 + 4 * levels,)),
         *[dma((2,))] * 4,
-        dma((2, far, 2)),
         dma((5,)),
         *[dma((2, far, parts))] * 2,
         dma((1 + nb,)),

time: 85.9 us -> 84.9 us (0.988)
  Pallas kernels: 84.9 us -> 83.7 us
    pallas_call x1, Pallas kernels: 84.1 us -> 82.9 us  [on_device(): pl.pallas_call(functools.partial(kernel, nb, zs), out_shape=(out, out, ou...]
where the time goes in v6:
time: 84.9 us; the launch traced here: 84.3 us
  Pallas kernels  83.7 us (99%)
    pallas_call x1, Pallas kernels, on_device(): pl.pallas_call(functools.partial(kernel, nb, zs), out_shape=(out, out, ou...  82.9 us

profile of v6, /device:TPU:1, one launch (start us, length us, event | category | flops | bytes accessed | tf_op | source)
XLA Modules:
  0.0 84.3 jit_solution(5806993776077175112)
XLA Ops:
  0.6 82.9 %shard_map.94 = (bf16[512,128]{1,0:T(8,128)(2,1)S(1)}, bf16[512,128]{1,0:T(8,128)(2,1)S(1)}, bf16[512,128]{1,0:T(8,128)(2,1)S(1)}) custom-call(bf16[512,128]{1,0:T(8,128)(2,1)} %refs_0_.1, bf16[3,128]{1,0:T(4,128)(2,1)} %refs_1_.1, bf16[8,8,64,128]{3,2,1,0:T(8,128)(2,1)} %refs_2_.1, s32[2,8]{1,0:T(2,128)} %refs_3_.1, bf16[1024,512]{1,0:T(8,128)(2,1)} %refs_4_.1, ...), custom_call_target="tpu_custom_call" | custom-call | tf_op jit(solution)/shard_map/pallas_call | solution.py:743
  83.6 0.8 shard_map.95

commit v7 on v6

--- a/solution.py
+++ b/solution.py
@@ -48,7 +48,7 @@
         x_v, cv, taps_ref, pattern, mixl, win, wout,
         halo, ghalo, st0, sx, st1, sy, wx, wy, wq,
         cot_all, cb1, cb_all, gb, mixed_all, hid, ga0, ga1, ga2, act, ghid,
-        rs_send, rs_recv, rs_own, ro_send, ro_recv, ro_own, term, grad_terms,
+        rs_send, rs_recv, rs_own, ro_send, ro_recv, ro_own, terms,
         g2, g1s, g1, g0s, g0, cross, out2, cs1, cs2, go_v,
         load_sem, save_sem, halo_sem, wx_sem, wq_sem, wr_sem, wz_sem, sx_sem, sy_sem,
         bx_sem, by_sem, ring_sem, cr_sem, mr_sem, ax_sem, ay_sem, cx_sem, cy_sem,
@@ -249,17 +249,16 @@
             arrival(self.buf.at[pl.ds(0, zs - 1)], self.send_sem.at[0])
 
     class Scatter:
-        def __init__(self, send, recv, own, send_sem, sems, pair, terms=None):
+        def __init__(self, send, recv, own, send_sem, sems, pair, terms, early):
             self.send, self.recv, self.own, self.send_sem, self.sems, self.pair = send, recv, own, send_sem, sems, pair
-            self.ahead = terms is not None
-            self.terms = terms
+            self.terms, self.early = terms, early
 
         def prepare(self, k):
             near = z if k == far else mod(z - k, zs)
             self.term(k)[...] = self.pair(mod(z + k, zs), near)
 
         def term(self, k):
-            return self.terms.at[far - k] if self.ahead else term
+            return self.terms.at[far - k]
 
         def at(self, way, step, p):
             slot = zs - 2 if step == 0 else 2 * (step - 1) + way
@@ -291,7 +290,7 @@
         def stage(self, k):
             step = far - k
             value_of = self.term(k)
-            if k == far or not self.ahead:
+            if k == far or (k == far - 1 and not self.early):
                 self.prepare(k)
             todo = [(way, p) for p in range(parts) for way in range(2)]
             if k == far:
@@ -299,7 +298,7 @@
             elif k == far - 1:
                 todo.sort(key=lambda item: ours(*item))
             for index, (way, p) in enumerate(todo):
-                if k == far - 1 and index == parts and self.ahead:
+                if k == far - 1 and index == parts:
                     for later in range(k - 1, 0, -1):
                         self.prepare(later)
                 value = value_of[pl.ds(p * lines_of, lines_of), pl.ds(0 if k == far else way * CH, CH)]
@@ -307,7 +306,7 @@
                 self.pass_on(way, step, p, value if came is None else value + came)
             if k == far:
                 self.own[...] = value_of[:, pl.ds(CH, CH)]
-                if self.ahead and far > 1:
+                if self.early and far > 1:
                     self.prepare(k - 1)
 
         def total(self, p):
@@ -615,8 +614,8 @@
             act[...], both(wout[:, channels(a)], wout[:, channels(b)], 1), preferred_element_type=F32
         )
 
-    grad_sum = Scatter(rs_send, rs_recv, rs_own, ring_sem.at[pl.ds(2, 1)], mr_sem, grad_pair, grad_terms)
-    out_sum = Scatter(ro_send, ro_recv, ro_own, ring_sem.at[pl.ds(3, 1)], cr_sem, out_pair)
+    grad_sum = Scatter(rs_send, rs_recv, rs_own, ring_sem.at[pl.ds(2, 1)], mr_sem, grad_pair, terms, True)
+    out_sum = Scatter(ro_send, ro_recv, ro_own, ring_sem.at[pl.ds(3, 1)], cr_sem, out_pair, terms, False)
     for k in range(far, 1, -1):
         grad_sum.stage(k)
     out_sum.stage(far)
@@ -719,7 +718,6 @@
         vmem((rows, CH), F32),
         *[vmem((zs - 1, *blocks), BF16)] * 2,
         vmem((rows, CH), F32),
-        vmem((rows, 2 * CH), F32),
         vmem((far, rows, 2 * CH), F32),
         *[vmem(blocks, BF16)] * 5,
         vmem(blocks, F32),

time: 84.9 us -> 85.7 us (level)
  no operation moved by 1% of the time
where the time goes in v7:
time: 85.7 us; the launch traced here: 84.8 us
  Pallas kernels  84.1 us (98%)
    pallas_call x1, Pallas kernels, on_device(): pl.pallas_call(functools.partial(kernel, nb, zs), out_shape=(out, out, ou...  83.4 us

profile of v7, /device:TPU:1, one launch (start us, length us, event | category | flops | bytes accessed | tf_op | source)
XLA Modules:
  0.0 84.8 jit_solution(5415673314173809251)
XLA Ops:
  0.6 83.4 %shard_map.94 = (bf16[512,128]{1,0:T(8,128)(2,1)S(1)}, bf16[512,128]{1,0:T(8,128)(2,1)S(1)}, bf16[512,128]{1,0:T(8,128)(2,1)S(1)}) custom-call(bf16[512,128]{1,0:T(8,128)(2,1)} %refs_0_.1, bf16[3,128]{1,0:T(4,128)(2,1)} %refs_1_.1, bf16[8,8,64,128]{3,2,1,0:T(8,128)(2,1)} %refs_2_.1, s32[2,8]{1,0:T(2,128)} %refs_3_.1, bf16[1024,512]{1,0:T(8,128)(2,1)} %refs_4_.1, ...), custom_call_target="tpu_custom_call" | custom-call | tf_op jit(solution)/shard_map/pallas_call | solution.py:741
  84.0 0.8 shard_map.95
